TPU v7x, 128 devices: a whole 4x4x4 slice. The times are simulated.
128 devices in a mesh: energy: 8 (over x, z_lo), momentum: 4 (over z_hi, core), atom: 4 (over y).
Axes of the slice: x: 4, y: 4, z: 4 (z_hi: 2, z_lo: 2; z = z_hi * 2 + z_lo), core: 2. Of those that a mesh axis runs over, the one named last changes fastest.
Arguments:
- green: bfloat16 [16, 32, 288, 1024], P('momentum', 'atom', None, 'energy'), may hold values from -6 to 6
- neighbours: int32 [32, 8], P('atom'), may hold values from 0 to 31, as said below
- offsets: int32 [16], replicated, may hold values from 1 to 32, as said below
- emit_weight: bfloat16 [16, 16], replicated, may hold values from 0.0099487305 to 0.099609375
- absorb_weight: bfloat16 [16, 16], replicated, may hold values from 0.0099487305 to 0.099609375
- coupling: bfloat16 [32, 8, 12, 12], P('atom'), may hold values from -1.75 to 1.75
Outputs:
- selfenergy: float32 [16, 32, 288, 1024], P('momentum', 'atom', None, 'energy')
Inputs may be any that keep to these rules, and one draw needn't show every extreme that they name: `neighbours`: every entry lies within 2 of its own atom index, and some entry lies exactly 2 above it. `offsets`: all entries are distinct, and one of them equals 32.
All inputs are finite; a program needn't handle non-finite values.
Results may differ from a plain program's by a relative error of at most 0.0041.
Values may be sent and summed in bfloat16 or wider, within the bound.
A program may use at most 128 MiB of HBM per device.

v0:
```python
import jax
import jax.numpy as jnp
from jax import lax
from jax.sharding import PartitionSpec as P

ORB = 12
NB = 8
SMAX = 32
REACH = 2


def with_halo(cells, sides, width):
    for axis, dim in sides:
        count = lax.axis_size(axis)
        ends = count - 1
        head = lax.slice_in_dim(cells, 0, width, axis=dim)
        tail = lax.slice_in_dim(cells, cells.shape[dim] - width, cells.shape[dim], axis=dim)
        cells = jnp.concatenate(
            [
                lax.ppermute(tail, axis, [(i, (i + 1) % count) for i in range(ends)]),
                cells,
                lax.ppermute(head, axis, [((i + 1) % count, i) for i in range(ends)]),
            ],
            axis=dim,
        )
    return cells


def shards(green, neighbours, offsets, emit_weight, absorb_weight, coupling):
    k_count, a_count, components, e_count = green.shape
    extended = with_halo(green, (("energy", 3),), SMAX)
    padded_len = e_count + 2 * SMAX
    k_total = k_count * lax.axis_size("momentum")
    k_first = lax.axis_index("momentum") * k_count
    source_pos = jnp.arange(padded_len)[None, :, None]
    target_pos = jnp.arange(e_count)[None, None, :]
    emit_pick = (source_pos == target_pos + SMAX - offsets[:, None, None]).astype(jnp.float32)
    absorb_pick = (source_pos == target_pos + SMAX + offsets[:, None, None]).astype(jnp.float32)
    emit_full = emit_weight.astype(jnp.float32)
    absorb_full = absorb_weight.astype(jnp.float32)
    block_piece = lax.all_gather(extended, "momentum", axis=0, tiled=True)
    sources = jnp.arange(block_piece.shape[0])
    targets = k_first + jnp.arange(k_count)
    lag_index = (targets[:, None] - sources[None, :]) % k_total
    lag_onehot = (lag_index[:, :, None] == jnp.arange(k_total)[None, None, :]).astype(jnp.float32)
    emit_coef = jnp.einsum("pqk,wk->pqw", lag_onehot, emit_full)
    absorb_coef = jnp.einsum("pqk,wk->pqw", lag_onehot, absorb_full)
    toeplitz_table = jnp.einsum("pqw,wfe->pqfe", emit_coef, emit_pick)
    toeplitz_table = toeplitz_table + jnp.einsum("pqw,wfe->pqfe", absorb_coef, absorb_pick)
    convolve_toeplitz_table = toeplitz_table.astype(jnp.bfloat16)
    hsum = jnp.einsum(
        "qacf,pqfe->pace", block_piece, convolve_toeplitz_table, preferred_element_type=jnp.float32
    ).astype(jnp.bfloat16)
    hsum = with_halo(hsum, (("atom", 1),), REACH)
    a_first = lax.axis_index("atom") * a_count - REACH
    local_index = neighbours - a_first
    blocks = hsum.reshape(k_count, a_count + 2 * REACH, 2, ORB, ORB, e_count)

    def add_slot(slot_index, accumulated):
        column = lax.dynamic_index_in_dim(local_index, slot_index, 1, keepdims=False)
        chosen = jnp.take(blocks, column, axis=1)
        coupling_slot = lax.dynamic_index_in_dim(coupling, slot_index, 1, keepdims=False)
        half_block = jnp.einsum(
            "aij,kacjle->kacile", coupling_slot, chosen, preferred_element_type=jnp.float32
        ).astype(jnp.bfloat16)
        return accumulated + jnp.einsum(
            "kacile,ajl->kacije", half_block, coupling_slot, preferred_element_type=jnp.float32
        )

    zeros_out = jnp.zeros((k_count, a_count, 2, ORB, ORB, e_count), jnp.float32)
    accumulated = lax.fori_loop(0, NB, add_slot, zeros_out)
    return accumulated.reshape(k_count, a_count, components, e_count)


def solution(mesh):
    in_specs = (
        P("momentum", "atom", None, "energy"),
        P("atom", None),
        P(),
        P(),
        P(),
        P("atom", None, None, None),
    )
    out_specs = P("momentum", "atom", None, "energy")
    return jax.shard_map(shards, mesh=mesh, in_specs=in_specs, out_specs=out_specs, check_vma=False)
```

profile of v0, /device:TPU:1, one launch (start us, length us, event | category | flops | bytes accessed | tf_op | source)
XLA Modules:
  0.0 374.6 jit_solution(17614420312330644482)
XLA Ops:
  6.5 4.6 %fusion.39 = (bf16[4,8,288,32]{3,2,1,0:T(8,128)(2,1)}, bf16[4,8,288,32]{3,2,1,0:T(8,128)(2,1)S(1)}) fusion(bf16[4,8,288,128]{3,2,1,0:T(8,128)(2,1)} %param.8), kind=kLoop, calls=%fused_computation.49 | loop fusion | bytes 2359296 | tf_op jit(solution)/shard_map/slice | solution.py:17
  11.1 2.3 copy.44
  13.4 5.3 %collective-permute-start = (bf16[4,8,288,32]{2,3,1,0:T(8,128)(2,1)S(1)}, bf16[4,8,288,32]{2,3,1,0:T(8,128)(2,1)}, u32[]{:S(2)}, u32[]{:S(2)}) collective-permute-start(bf16[4,8,288,32]{2,3,1,0:T(8,128)(2,1)S(1)} %copy.44), channel_id=1, source_target_pairs={{0,16},{16,32},{32,48},{48,64},{64,80},{80,96},{96,112},{1,17},{17... | collective-permute-start | bytes 1769480 | tf_op jit(solution)/shard_map/ppermute | solution.py:20
  18.7 1.8 copy.45
  21.9 28.9 %collective-permute-done = bf16[4,8,288,32]{2,3,1,0:T(8,128)(2,1)} collective-permute-done((bf16[4,8,288,32]{2,3,1,0:T(8,128)(2,1)S(1)}, bf16[4,8,288,32]{2,3,1,0:T(8,128)(2,1)}, u32[]{:S(2)}, u32[]{:S(2)}) %collective-permute-start) | collective-permute-done | bytes 589856 | tf_op jit(solution)/shard_map/ppermute | solution.py:20
  50.9 2.8 copy.27
  53.7 2.8 copy.29
  56.5 6.1 %pad_maximum_fusion = bf16[4,8,288,192]{3,2,0,1:T(8,128)(2,1)} fusion(bf16[4,8,288,32]{3,2,0,1:T(8,128)(2,1)} %copy.29, bf16[4,8,288,32]{3,2,0,1:T(8,128)(2,1)} %copy.27, bf16[4,8,288,128]{3,2,1,0:T(8,128)(2,1)S(1)} %copy-done.4), kind=kLoop, calls=%fused_computation.18 | loop fusion | flops 10616832 | bytes 7077888 | tf_op jit(solution)/shard_map/concatenate | solution.py:18
  63.5 3.8 %fusion.23 = f32[4,16,192,128]{3,1,2,0:T(8,128)} fusion(s32[16,128]{1,0:T(8,128)S(1)} %get-tuple-element.150, s32[4,16]{1,0:T(4,128)S(1)} %add_select_fusion, bf16[16,16]{1,0:T(8,128)(2,1)S(1)} %copy-done), kind=kOutput, calls=%fused_computation.28 | convolution fusion | flops 50758656 | bytes 6300416 | tf_op jit(solution)/shard_map/pqw,wfe->pqfe/dot_general | solution.py:48
  67.3 123.9 %all-gather.2.cloned.1.call-done = bf16[16,8,288,192]{3,2,0,1:T(8,128)(2,1)} async-done(((bf16[4,8,288,192]{3,2,0,1:T(8,128)(2,1)}), bf16[16,8,288,192]{3,2,0,1:T(8,128)(2,1)}) %all-gather.2.cloned.1.call-update) | async-done | bytes 14155792 | tf_op jit(solution)/shard_map/all_gather | solution.py:41
  191.2 29.7 %copy.40 = bf16[16,8,288,192,1]{2,0,3,1,4:T(8,128)(2,1)} copy(bf16[16,8,288,192,1]{3,2,0,1,4:T(8,128)(2,1)} %bitcast.75) | data formatting | bytes 28311552 | tf_op jit(solution)/shard_map/all_gather | solution.py:41
  220.9 15.0 %fusion.17 = bf16[4,8,288,128]{3,2,1,0:T(8,128)(2,1)S(1)} fusion(bf16[16,8,288,192,1]{2,0,3,1,4:T(8,128)(2,1)} %copy.40, f32[4,16,192,128]{3,1,2,0:T(8,128)} %fusion.23, bf16[4,16,16,1]{2,1,3,0:T(8,128)(2,1)S(1)} %convolution_bitcast_fusion, s32[16,128]{1,0:T(8,128)S(1)} %get-tuple-element.149), kind=kOutput, calls=%fused_computation.23 | convolution fusion | flops 7302807552 | bytes 22816768 | tf_op jit(solution)/shard_map/qacf,pqfe->pace/dot_general | solution.py:51
  237.0 3.1 collective-permute-start.2
  241.8 11.1 %collective-permute-done.2 = bf16[4,2,288,128]{3,2,1,0:T(8,128)(2,1)S(1)} collective-permute-done((bf16[4,2,288,128]{3,2,1,0:T(8,128)(2,1)}, bf16[4,2,288,128]{3,2,1,0:T(8,128)(2,1)S(1)}, u32[]{:S(2)}, u32[]{:S(2)}) %collective-permute-start.2) | collective-permute-done | bytes 589856 | tf_op jit(solution)/shard_map/ppermute | solution.py:20
  252.8 3.9 %collective-permute-done.3 = bf16[4,2,288,128]{3,2,1,0:T(8,128)(2,1)} collective-permute-done((bf16[4,2,288,128]{3,2,1,0:T(8,128)(2,1)}, bf16[4,2,288,128]{3,2,1,0:T(8,128)(2,1)}, u32[]{:S(2)}, u32[]{:S(2)}) %collective-permute-start.3) | collective-permute-done | bytes 589856 | tf_op jit(solution)/shard_map/ppermute | solution.py:22
  258.1 2.7 copy.31
  260.9 3.5 copy.33
  264.3 94.9 %while.14 = (s32[]{:T(128)}, f32[4,8,2,12,12,128]{5,4,3,2,0,1:T(8,128)}, bf16[8,8,12,12]{3,2,0,1:T(8,128)(2,1)S(1)}, s32[8,8]{0,1:T(8,128)S(1)}, bf16[4,12,2,12,...) while((s32[]{:T(128)}, f32[4,8,2,12,12,128]{5,4,3,2,0,1:T(8,128)}, ...), condition=%wide.region_1.2_spmd.clone, body=%wide.region_0.1_spmd.clone.sunk | while | flops 61342768 | bytes 66916656 | solution.py:71
  264.4 3.5 gather_fusion
  271.0 2.5 bitcast_add_fusion.2
  273.5 2.7 copy-done.3
  276.2 3.5 gather_fusion
  281.1 1.8 copy-done.2
  282.9 2.5 bitcast_add_fusion.2
  285.4 2.7 copy-done.3
  288.1 3.5 gather_fusion
  292.9 1.8 copy-done.2
  294.7 2.5 bitcast_add_fusion.2
  297.3 2.7 copy-done.3
  299.9 3.5 gather_fusion
  306.6 2.5 bitcast_add_fusion.2
  309.1 2.7 copy-done.3
  311.8 3.5 gather_fusion
  316.7 1.8 copy-done.2
  318.5 2.5 bitcast_add_fusion.2
  321.0 2.7 copy-done.3
  323.7 3.5 gather_fusion
  330.3 2.5 bitcast_add_fusion.2
  332.9 2.7 copy-done.3
  335.5 3.5 gather_fusion
  342.2 2.5 bitcast_add_fusion.2
  344.7 2.7 copy-done.3
  347.4 3.5 gather_fusion
  352.3 1.8 copy-done.2
  354.1 2.5 bitcast_add_fusion.2
  356.6 2.7 copy-done.3
  359.3 5.5 %copy.34 = f32[4,8,2,12,12,128]{5,1,4,3,2,0:T(8,128)S(1)} copy(f32[4,8,2,12,12,128]{5,4,3,2,0,1:T(8,128)} %get-tuple-element.99) | data formatting | bytes 9437184 | tf_op jit(solution)/shard_map/while | solution.py:71
  364.8 3.0 copy.35
  (82 shorter events, 24.5 us)
Async XLA Ops:
  6.5 57.0 %copy-start = (bf16[16,16]{1,0:T(8,128)(2,1)S(1)}, bf16[16,16]{1,0:T(8,128)(2,1)}, u32[]{:S(2)}) copy-start(bf16[16,16]{1,0:T(8,128)(2,1)} %param.11) | copy-start | bytes 1540
  6.5 184.7 %all-gather.2.cloned.1.call-start = ((), (), s32[]{:S(2)}) async-start(), calls=%async_computation | async-start | bytes 23592960 | tf_op jit(solution)/shard_map/all_gather | solution.py:41
  13.4 37.4 %collective-permute-start = (bf16[4,8,288,32]{2,3,1,0:T(8,128)(2,1)S(1)}, bf16[4,8,288,32]{2,3,1,0:T(8,128)(2,1)}, u32[]{:S(2)}, u32[]{:S(2)}) collective-permute-start(bf16[4,8,288,32]{2,3,1,0:T(8,128)(2,1)S(1)} %copy.44), channel_id=1, source_target_pairs={{0,16},{16,32},{32,48},{48,64},{64,80},{80,96},{96,112},{1,17},{17... | collective-permute-start | bytes 1769480 | tf_op jit(solution)/shard_map/ppermute | solution.py:20
  20.5 36.0 %copy-start.4 = (bf16[4,8,288,128]{3,2,1,0:T(8,128)(2,1)S(1)}, bf16[4,8,288,128]{3,2,1,0:T(8,128)(2,1)}, u32[]{:S(2)}) copy-start(bf16[4,8,288,128]{3,2,1,0:T(8,128)(2,1)} %param.8) | copy-start | bytes 7077892
  20.5 33.2 %collective-permute-start.1 = (bf16[4,8,288,32]{2,3,1,0:T(8,128)(2,1)}, bf16[4,8,288,32]{2,3,1,0:T(8,128)(2,1)}, u32[]{:S(2)}, u32[]{:S(2)}) collective-permute-start(bf16[4,8,288,32]{2,3,1,0:T(8,128)(2,1)} %copy.45), channel_id=1, source_target_pairs={{16,0},{32,16},{48,32},{64,48},{80,64},{96,80},{112,96},{17,1},{33... | collective-permute-start | bytes 1769480 | tf_op jit(solution)/shard_map/ppermute | solution.py:22
  62.6 0.7 copy-start.8
  62.6 0.9 copy-start.7
  220.9 20.7 %copy-start.6 = (s32[8,8]{1,0:T(8,128)S(1)}, s32[8,8]{1,0:T(8,128)}, u32[]{:S(2)}) copy-start(s32[8,8]{1,0:T(8,128)} %param.9) | copy-start | bytes 772
  220.9 20.8 %copy-start.5 = (bf16[8,8,12,12]{3,1,2,0:T(8,128)(2,1)S(1)}, bf16[8,8,12,12]{3,1,2,0:T(8,128)(2,1)}, u32[]{:S(2)}) copy-start(bf16[8,8,12,12]{3,1,2,0:T(8,128)(2,1)} %param.13) | copy-start | bytes 55300
  237.0 15.8 %collective-permute-start.2 = (bf16[4,2,288,128]{3,2,1,0:T(8,128)(2,1)}, bf16[4,2,288,128]{3,2,1,0:T(8,128)(2,1)S(1)}, u32[]{:S(2)}, u32[]{:S(2)}) collective-permute-start(bf16[4,2,288,128]{3,2,1,0:T(8,128)(2,1)} %get-tuple-element.145), channel_id=1, source_target_pairs={{0,1},{1,2},{2,3},{4,5},{5,6},{6,7},{8,9},{9,10},{10,11},{12,13},{... | collective-permute-start | bytes 1769480 | tf_op jit(solution)/shard_map/ppermute | solution.py:20
  240.1 16.6 %collective-permute-start.3 = (bf16[4,2,288,128]{3,2,1,0:T(8,128)(2,1)}, bf16[4,2,288,128]{3,2,1,0:T(8,128)(2,1)}, u32[]{:S(2)}, u32[]{:S(2)}) collective-permute-start(bf16[4,2,288,128]{3,2,1,0:T(8,128)(2,1)} %get-tuple-element.146), channel_id=1, source_target_pairs={{1,0},{2,1},{3,2},{5,4},{6,5},{7,6},{9,8},{10,9},{11,10},{13,12},{... | collective-permute-start | bytes 1769480 | tf_op jit(solution)/shard_map/ppermute | solution.py:22
  268.2 2.8 copy-start.2
  273.5 2.7 copy-start.3
  280.1 2.8 copy-start.2
  285.4 2.7 copy-start.3
  292.0 2.8 copy-start.2
  297.3 2.7 copy-start.3
  303.8 2.8 copy-start.2
  309.1 2.7 copy-start.3
  315.7 2.8 copy-start.2
  321.0 2.7 copy-start.3
  327.6 2.8 copy-start.2
  332.9 2.7 copy-start.3
  339.4 2.8 copy-start.2
  344.7 2.7 copy-start.3
  351.3 2.8 copy-start.2
  356.6 2.7 copy-start.3
  364.7 3.0 copy-start.1
Sparse Core Ops, SparseCore 0:
  62.7 128.4 all-gather.1
where the time goes:
time: 376 us; the launch traced here: 375 us
  waiting for transfers between devices  168 us (45%)
  local copies, waits for them, and re-layouts  124 us (33%)
  matrix products  46.7 us (12%)
  between operations  13.5 us (4%)
  starting transfers between devices  11.3 us (3%)
  other arithmetic  10.7 us (3%)
    all_gather x1, waiting for transfers between devices, shards(): block_piece = lax.all_gather(extended, 'momentum', axis=0, tiled=True)  124 us
    ppermute x2, waiting for transfers between devices, with_halo(): lax.ppermute(tail, axis, [(i, (i + 1) % count) for i in range(ends)])  40 us
    while x32, local copies, waits for them, and re-layouts  35.7 us
    all_gather x1, local copies, waits for them, and re-layouts, shards(): block_piece = lax.all_gather(extended, 'momentum', axis=0, tiled=True)  29.7 us
    gather x8, local copies, waits for them, and re-layouts, add_slot(): chosen = jnp.take(blocks, column, axis=1)  27.9 us
    dot_general x8, matrix products, add_slot(): jnp.einsum('kacile,ajl->kacije', half_block, coupling_slot, preferred_ele...  20 us
    dot_general x1, matrix products, shards(): jnp.einsum('qacf,pqfe->pace', block_piece, convolve_toeplitz_table, prefe...  15 us
    ppermute x2, starting transfers between devices, with_halo(): lax.ppermute(tail, axis, [(i, (i + 1) % count) for i in range(ends)])  8.4 us
  transfers between devices with their start and end apart: 5, of which 4 were waited for; matrix products, arithmetic and copies ran while one was open for 2% of the time, Pallas kernels for 0%

commit v1 on v0

v1 whole, which is shorter than its diff:
```python
import functools

import jax
import jax.numpy as jnp
from jax import lax
from jax.experimental import pallas as pl
from jax.experimental.pallas import tpu as pltpu
from jax.sharding import PartitionSpec as P

ORB = 12
NB = 8
SMAX = 32
REACH = 2
KPTS = 16
PAIR = ORB * ORB
LANES = 128
SPAN = 2 * REACH + 1
MESH = pl.DeviceIdType.MESH
BF = jnp.bfloat16
F32 = jnp.float32


def place():
    e = lax.axis_index("energy")
    m = lax.axis_index("momentum")
    return e // 2, e % 2, m // 2, m % 2


def partner(t, u):
    _, zl, zh, core = place()
    far = 1 - t // 2
    flip = ((t + 1) // 2) % 2
    zh_t = zh + far * (1 - 2 * zh)
    core_t = core + flip * (1 - 2 * core)
    zl_t = zl + u * (1 - 2 * zl)
    return zh_t * 2 + core_t, zl_t


def share(chunk, m, zl):
    if chunk == 0:
        return m + 4 * (m // 2), zl
    return m + 2, zl


def exchange_kernel(
    green, offsets, emit, absorb, coupling, near,
    hout, kout,
    arrived, made, left, right, left_out, right_out,
    base, t_main, t_left, t_right, pack, kacc,
    in_send, in_recv, in_local, x_send, x_recv, out_send, out_recv, out_local, y_send, y_recv, k_sem,
):
    x, zl, zh, core = place()
    m = zh * 2 + core
    y = lax.axis_index("atom")

    def at(m_to, zl_to):
        return {"energy": x * 2 + zl_to, "momentum": m_to}

    x_left = {"energy": ((x + 3) % 4) * 2 + zl}
    x_right = {"energy": ((x + 1) % 4) * 2 + zl}
    y_left = {"atom": (y + 3) % 4}
    y_right = {"atom": (y + 1) % 4}

    barrier = pltpu.get_barrier_semaphore()
    steps = [(t, u) for t in range(4) for u in range(2) if (t, u) != (3, 0)]
    for t, u in steps:
        m_to, zl_to = partner(t, u)
        pl.semaphore_signal(barrier, inc=1, device_id=at(m_to, zl_to), device_id_type=MESH)
    for side in (x_left, x_right, y_left, y_right):
        pl.semaphore_signal(barrier, inc=1, device_id=side, device_id_type=MESH)
    pl.semaphore_wait(barrier, len(steps) + 4)

    def rows(block):
        return pl.ds(pl.multiple_of(block * PAIR, 16), PAIR)

    def send_in(chunk, t, u):
        m_to, zl_to = partner(t, u)
        atom, c = share(chunk, m_to, zl_to)
        return pltpu.make_async_remote_copy(
            src_ref=green.at[:, atom, c],
            dst_ref=arrived.at[chunk, pl.ds(m * 4, 4), rows(zl), :],
            send_sem=in_send.at[chunk, t, u],
            recv_sem=in_recv.at[chunk, t, u],
            device_id=at(m_to, zl_to),
            device_id_type=MESH,
        )

    def own_in(chunk):
        atom, c = share(chunk, m, zl)
        return pltpu.make_async_copy(
            green.at[:, atom, c], arrived.at[chunk, pl.ds(m * 4, 4), rows(zl), :], in_local.at[chunk]
        )

    for chunk in range(2):
        for t, u in steps:
            send_in(chunk, t, u).start()
        own_in(chunk).start()

    lane = lax.broadcasted_iota(jnp.int32, (KPTS, 2 * LANES), 1)
    emit_pick = (lane == offsets[...]).astype(BF)
    absorb_pick = (lane == 2 * LANES - offsets[...]).astype(BF)
    dims = (((0,), (0,)), ((), ()))
    base[...] = lax.dot_general(emit[...], emit_pick, dims, preferred_element_type=F32) + lax.dot_general(
        absorb[...], absorb_pick, dims, preferred_element_type=F32
    )
    span = LANES + 2 * SMAX

    @pl.loop(0, KPTS)
    def _(lag):
        row = jnp.broadcast_to(base[pl.ds(lag, 1), :], (span, 2 * LANES))
        block = pltpu.roll(row, 2 * LANES - SMAX, 1, stride=1, stride_axis=0)[:, :LANES].astype(BF)
        for half in range(2):
            r = (2 * KPTS + half - lag) % KPTS
            for again in range(2):
                slot = r + KPTS * again
                cols = pl.ds(half * LANES, LANES)
                t_left[pl.ds(pl.multiple_of(slot * SMAX, SMAX), SMAX), cols] = block[:SMAX]
                t_main[pl.ds(pl.multiple_of(slot * LANES, LANES), LANES), cols] = block[SMAX : SMAX + LANES]
                t_right[pl.ds(pl.multiple_of(slot * SMAX, SMAX), SMAX), cols] = block[SMAX + LANES :]

    src = lax.broadcasted_iota(jnp.int32, (4 * LANES, 2 * LANES), 0)
    dst = lax.broadcasted_iota(jnp.int32, (4 * LANES, 2 * LANES), 1)
    inner = dst % LANES
    wanted = (inner // SMAX) * LANES + inner % SMAX + (dst // LANES) * (LANES - SMAX)
    pack[...] = (src == wanted).astype(BF)

    prow = lax.broadcasted_iota(jnp.int32, (PAIR, ORB), 0)
    pcol = lax.broadcasted_iota(jnp.int32, (PAIR, ORB), 1)
    up_major = (prow // ORB == pcol).astype(BF)
    up_minor = (prow % ORB == pcol).astype(BF)
    qrow = lax.broadcasted_iota(jnp.int32, (ORB, PAIR), 0)
    qcol = lax.broadcasted_iota(jnp.int32, (ORB, PAIR), 1)
    across_major = (qcol // ORB == qrow).astype(BF)
    across_minor = (qcol % ORB == qrow).astype(BF)

    @pl.loop(0, 8)
    def _(a):
        totals = [jnp.zeros((PAIR, PAIR), F32) for _ in range(SPAN)]
        for n in range(NB):
            block = coupling[a, n]
            first = jnp.dot(block, across_major, preferred_element_type=F32).astype(BF)
            second = jnp.dot(block, across_minor, preferred_element_type=F32).astype(BF)
            first = jnp.dot(up_major, first, preferred_element_type=F32)
            second = jnp.dot(up_minor, second, preferred_element_type=F32)
            product = first * second
            step = near[a, n] - (a + y * 8) + REACH
            for d in range(SPAN):
                totals[d] = totals[d] + product * (step == d).astype(F32)
        kacc[a] = jnp.concatenate(totals, axis=1).astype(BF)

    k_copy = pltpu.make_async_copy(kacc, kout, k_sem)
    k_copy.start()

    keep_left = (x > 0).astype(F32)
    keep_right = (x < 3).astype(F32)

    def edge_copies(chunk):
        to_left = pltpu.make_async_remote_copy(
            src_ref=left_out.at[chunk], dst_ref=right.at[chunk, :, pl.ds(PAIR, PAIR), :],
            send_sem=x_send.at[chunk, 0], recv_sem=x_recv.at[chunk, 0],
            device_id=x_left, device_id_type=MESH,
        )
        to_right = pltpu.make_async_remote_copy(
            src_ref=right_out.at[chunk], dst_ref=left.at[chunk, :, pl.ds(0, PAIR), :],
            send_sem=x_send.at[chunk, 1], recv_sem=x_recv.at[chunk, 1],
            device_id=x_right, device_id_type=MESH,
        )
        return to_left, to_right

    def send_out(chunk, t, u):
        m_to, zl_to = partner(t, u)
        atom, c = share(chunk, m, zl)
        return pltpu.make_async_remote_copy(
            src_ref=made.at[chunk, pl.ds(m_to * 4, 4), rows(zl_to), :],
            dst_ref=hout.at[:, c, atom + REACH],
            send_sem=out_send.at[chunk, t, u],
            recv_sem=out_recv.at[chunk, t, u],
            device_id=at(m_to, zl_to),
            device_id_type=MESH,
        )

    def own_out(chunk):
        atom, c = share(chunk, m, zl)
        return pltpu.make_async_copy(
            made.at[chunk, pl.ds(m * 4, 4), rows(zl), :], hout.at[:, c, atom + REACH], out_local.at[chunk]
        )

    for chunk in range(2):
        for t, u in steps:
            send_in(chunk, t, u).wait_recv()
        own_in(chunk).wait()

        for group in range(4):
            four = jnp.concatenate([arrived[chunk, group * 4 + i] for i in range(4)], axis=1)
            packed = jnp.dot(four, pack[...], preferred_element_type=F32)
            left_out[chunk, group] = (packed[:PAIR, :LANES] * keep_left).astype(BF)
            left[chunk, group, PAIR:, :] = packed[:PAIR, LANES:].astype(BF)
            right[chunk, group, :PAIR, :] = packed[PAIR:, :LANES].astype(BF)
            right_out[chunk, group] = (packed[PAIR:, LANES:] * keep_right).astype(BF)
        edges = edge_copies(chunk)
        for copy in edges:
            copy.start()
        for copy in edges:
            copy.wait()

        @pl.loop(0, 4)
        def _(t):
            m_to, _ = partner(t, 0)

            @pl.loop(0, 2)
            def _(half):
                kp = m_to * 2 + half
                start = KPTS - 2 * kp
                main = jnp.concatenate([arrived[chunk, q] for q in range(KPTS)], axis=1)
                total = jnp.dot(
                    main, t_main[pl.ds(pl.multiple_of(start * LANES, LANES), KPTS * LANES), :],
                    preferred_element_type=F32,
                )
                window = pl.ds(pl.multiple_of(start * SMAX, SMAX), KPTS * SMAX)
                lows = jnp.concatenate([left[chunk, g] for g in range(4)], axis=1)
                total = total + jnp.dot(lows, t_left[window, :], preferred_element_type=F32)
                highs = jnp.concatenate([right[chunk, g] for g in range(4)], axis=1)
                total = total + jnp.dot(highs, t_right[window, :], preferred_element_type=F32)
                total = total.astype(BF)
                made[chunk, 2 * kp] = total[:, :LANES]
                made[chunk, 2 * kp + 1] = total[:, LANES:]

            send_out(chunk, t, 1).start()

            @pl.when(t < 3)
            def _():
                send_out(chunk, t, 0).start()

        own_out(chunk).start()

    def y_copies():
        down = pltpu.make_async_remote_copy(
            src_ref=hout.at[:, :, pl.ds(REACH, REACH)], dst_ref=hout.at[:, :, pl.ds(8 + REACH, REACH)],
            send_sem=y_send.at[0], recv_sem=y_recv.at[0], device_id=y_left, device_id_type=MESH,
        )
        up = pltpu.make_async_remote_copy(
            src_ref=hout.at[:, :, pl.ds(8, REACH)], dst_ref=hout.at[:, :, pl.ds(0, REACH)],
            send_sem=y_send.at[1], recv_sem=y_recv.at[1], device_id=y_right, device_id_type=MESH,
        )
        return down, up

    for t, u in steps:
        send_out(0, t, u).wait_recv()
    own_out(0).wait()
    halos = y_copies()
    for copy in halos:
        copy.start()
    for t, u in steps:
        send_out(1, t, u).wait_recv()
    own_out(1).wait()
    for copy in halos:
        copy.wait()
    k_copy.wait()
    for chunk in range(2):
        for t, u in steps:
            send_in(chunk, t, u).wait_send()
            send_out(chunk, t, u).wait_send()


def apply_kernel(h_ref, k_ref, o_ref):
    a = pl.program_id(1)
    four = [h_ref[k, 0, pl.ds(a, SPAN)].reshape(SPAN * PAIR, LANES) for k in range(4)]
    total = jnp.dot(k_ref[0], jnp.concatenate(four, axis=1), preferred_element_type=F32)
    for k in range(4):
        o_ref[k, 0, 0] = total[:, k * LANES : (k + 1) * LANES]


def shards(green, neighbours, offsets, emit_weight, absorb_weight, coupling):
    k_count, a_count, components, e_count = green.shape
    extended = a_count + 2 * REACH
    vmem = pl.BlockSpec(memory_space=pltpu.VMEM)
    hbm = pl.BlockSpec(memory_space=pl.ANY)
    dma = pltpu.SemaphoreType.DMA
    span = LANES + 2 * SMAX
    hsum, kron = pl.pallas_call(
        exchange_kernel,
        out_shape=(
            jax.ShapeDtypeStruct((k_count, 2, extended, PAIR, LANES), BF),
            jax.ShapeDtypeStruct((a_count, PAIR, SPAN * PAIR), BF),
        ),
        in_specs=[hbm, vmem, vmem, vmem, vmem, pl.BlockSpec(memory_space=pltpu.SMEM)],
        out_specs=(hbm, hbm),
        scratch_shapes=[
            pltpu.VMEM((2, KPTS, 2 * PAIR, LANES), BF),
            pltpu.VMEM((2, KPTS, 2 * PAIR, LANES), BF),
            pltpu.VMEM((2, 4, 2 * PAIR, LANES), BF),
            pltpu.VMEM((2, 4, 2 * PAIR, LANES), BF),
            pltpu.VMEM((2, 4, PAIR, LANES), BF),
            pltpu.VMEM((2, 4, PAIR, LANES), BF),
            pltpu.VMEM((KPTS, 2 * LANES), F32),
            pltpu.VMEM((2 * KPTS * LANES, 2 * LANES), BF),
            pltpu.VMEM((2 * KPTS * SMAX, 2 * LANES), BF),
            pltpu.VMEM((2 * KPTS * SMAX, 2 * LANES), BF),
            pltpu.VMEM((4 * LANES, 2 * LANES), BF),
            pltpu.VMEM((a_count, PAIR, SPAN * PAIR), BF),
            dma((2, 4, 2)), dma((2, 4, 2)), dma((2,)),
            dma((2, 2)), dma((2, 2)),
            dma((2, 4, 2)), dma((2, 4, 2)), dma((2,)),
            dma((2,)), dma((2,)), dma,
        ],
        compiler_params=pltpu.CompilerParams(
            collective_id=0, has_side_effects=True, vmem_limit_bytes=48 * 1024 * 1024
        ),
        name="exchange",
    )(
        green.reshape(k_count, a_count, 2, PAIR, e_count),
        offsets.reshape(KPTS, 1),
        emit_weight,
        absorb_weight,
        coupling,
        neighbours,
    )
    out = pl.pallas_call(
        apply_kernel,
        grid=(2, a_count),
        out_shape=jax.ShapeDtypeStruct((k_count, a_count, 2, PAIR, e_count), F32),
        in_specs=[
            pl.BlockSpec((k_count, 1, extended, PAIR, LANES), lambda c, a: (0, c, 0, 0, 0)),
            pl.BlockSpec((1, PAIR, SPAN * PAIR), lambda c, a: (a, 0, 0)),
        ],
        out_specs=pl.BlockSpec((k_count, 1, 1, PAIR, LANES), lambda c, a: (0, a, c, 0, 0)),
        compiler_params=pltpu.CompilerParams(vmem_limit_bytes=32 * 1024 * 1024),
        name="apply",
    )(hsum, kron)
    return out.reshape(k_count, a_count, components, e_count)


def solution(mesh):
    in_specs = (
        P("momentum", "atom", None, "energy"),
        P("atom", None),
        P(),
        P(),
        P(),
        P("atom", None, None, None),
    )
    out_specs = P("momentum", "atom", None, "energy")
    return jax.shard_map(shards, mesh=mesh, in_specs=in_specs, out_specs=out_specs, check_vma=False)
```

time: 376 us -> 81.3 us (0.22)
  waiting for transfers between devices: 168 us -> 0 us
  local copies, waits for them, and re-layouts: 124 us -> 7.42 us
  Pallas kernels: 0 us -> 73.5 us
  matrix products: 46.7 us -> 0 us
  between operations: 13.5 us -> 0.04 us
  starting transfers between devices: 11.3 us -> 0 us
  other arithmetic: 10.7 us -> 0 us
    all_gather x1 -> x0, waiting for transfers between devices: 124 us -> none  [shards(): block_piece = lax.all_gather(extended, 'momentum', axis=0, tiled=True)]
    pallas_call x0 -> x2, Pallas kernels: none -> 73.5 us  [the longest x1 65 us: shards(): pl.pallas_call(exchange_kernel, out_shape=(jax.ShapeDtypeStruct((k_count,...]
    dot_general x19 -> x0, matrix products: 46.7 us -> none  [the longest x8 20 us: add_slot(): jnp.einsum('kacile,ajl->kacije', half_block, coupling_slot, preferred_ele...]
    ppermute x4 -> x0, waiting for transfers between devices: 43.8 us -> none  [the longest x2 40 us: with_halo(): lax.ppermute(tail, axis, [(i, (i + 1) % count) for i in range(ends)])]
    while x33 -> x0, local copies, waits for them, and re-layouts: 41.2 us -> none
    all_gather x1 -> x0, local copies, waits for them, and re-layouts: 29.7 us -> none  [shards(): block_piece = lax.all_gather(extended, 'momentum', axis=0, tiled=True)]
    gather x8 -> x0, local copies, waits for them, and re-layouts: 27.9 us -> none  [add_slot(): chosen = jnp.take(blocks, column, axis=1)]
    ppermute x4 -> x0, starting transfers between devices: 11.3 us -> none  [the longest x2 8.4 us: with_halo(): lax.ppermute(tail, axis, [(i, (i + 1) % count) for i in range(ends)])]
  transfers between devices with their start and end apart: 5 -> 0, of which waited for: 4 -> 0; matrix products, arithmetic and copies ran while one was open for 2% -> 0% of each run, Pallas kernels for 0% -> 0%
where the time goes in v1:
time: 81.3 us; the launch traced here: 81 us
  Pallas kernels  73.5 us (90%)
  local copies, waits for them, and re-layouts  7.42 us (9%)
    pallas_call x1, Pallas kernels, shards(): pl.pallas_call(exchange_kernel, out_shape=(jax.ShapeDtypeStruct((k_count,...  65 us
    pallas_call x1, Pallas kernels, shards(): pl.pallas_call(apply_kernel, grid=(2, a_count), out_shape=jax.ShapeDtypeS...  8.56 us
    unnamed x11, local copies, waits for them, and re-layouts  6.69 us

profile of v1, /device:TPU:1, one launch (start us, length us, event | category | flops | bytes accessed | tf_op | source)
XLA Modules:
  0.0 81.0 jit_solution(47778561940337601)
XLA Ops:
  0.0 0.7 copy.7.offsets
  0.7 1.0 %copy.8.coupling = bf16[8,8,12,12]{3,2,1,0:T(8,128)(2,1)S(1)} copy(bf16[8,8,12,12]{3,1,2,0:T(8,128)(2,1)} %param.11) | data formatting | bytes 36864 | tf_op args[5]
  1.7 0.0 copy-start.1
  1.7 1.7 %copy-done.1 = bf16[4,8,288,128]{3,2,1,0:T(8,128)(2,1)S(1)} copy-done((bf16[4,8,288,128]{3,2,1,0:T(8,128)(2,1)S(1)}, bf16[4,8,288,128]{3,2,1,0:T(8,128)(2,1)}, u32[]{:S(2)}) %copy-start.1) | copy-done | bytes 2359320
  3.4 0.0 copy-start.2
  3.4 0.7 copy-done.2
  4.1 0.0 copy-start.3
  4.1 0.7 copy-done.3
  4.8 0.0 copy-start.4
  4.8 0.7 copy-done.4
  5.4 65.0 %exchange.1 = (bf16[4,2,12,144,128]{4,3,2,1,0:T(8,128)(2,1)}, bf16[8,144,720]{2,1,0:T(8,128)(2,1)S(1)}) custom-call(bf16[4,8,2,144,128]{4,3,2,1,0:T(8,128)(2,1)S(1)} %bitcast.3, s32[16,1]{1,0:T(8,128)S(1)} %copy.7.offsets, bf16[16,16]{1,0:T(8,128)(2,1)S(1)} %copy-done.2, bf16[16,16]{1,0:T(8,128)(2,1)S(1)} %copy-done.3, ...), custom_call_target="tpu_custom_call" | custom-call | tf_op jit(solution)/shard_map/exchange/pallas_call | solution.py:280
  70.4 0.0 copy-start
  70.4 2.0 %copy-done = bf16[4,2,12,144,128]{4,3,2,1,0:T(8,128)(2,1)S(1)} copy-done((bf16[4,2,12,144,128]{4,3,2,1,0:T(8,128)(2,1)S(1)}, bf16[4,2,12,144,128]{4,3,2,1,0:T(8,128)(2,1)}, u32[]{:S(2)}) %copy-start) | copy-done | bytes 3538968
  72.4 8.6 %apply.1 = f32[4,8,2,144,128]{4,3,2,1,0:T(8,128)} custom-call(bf16[4,2,12,144,128]{4,3,2,1,0:T(8,128)(2,1)S(1)} %copy-done, bf16[8,144,720]{2,1,0:T(8,128)(2,1)S(1)} %get-tuple-element.8.k_ref), custom_call_target="tpu_custom_call" | custom-call | tf_op jit(solution)/shard_map/apply/pallas_call | solution.py:318
Async XLA Ops:
  1.7 1.7 %copy-start.1 = (bf16[4,8,288,128]{3,2,1,0:T(8,128)(2,1)S(1)}, bf16[4,8,288,128]{3,2,1,0:T(8,128)(2,1)}, u32[]{:S(2)}) copy-start(bf16[4,8,288,128]{3,2,1,0:T(8,128)(2,1)} %param.6) | copy-start | bytes 7077892
  3.4 0.7 copy-start.2
  4.1 0.7 copy-start.3
  4.8 0.7 copy-start.4
  70.4 2.0 %copy-start = (bf16[4,2,12,144,128]{4,3,2,1,0:T(8,128)(2,1)S(1)}, bf16[4,2,12,144,128]{4,3,2,1,0:T(8,128)(2,1)}, u32[]{:S(2)}) copy-start(bf16[4,2,12,144,128]{4,3,2,1,0:T(8,128)(2,1)} %get-tuple-element.7.h_ref) | copy-start | bytes 10616836

commit v2 on v1

v2 whole, which is shorter than its diff:
```python
import functools

import jax
import jax.numpy as jnp
from jax import lax
from jax.experimental import pallas as pl
from jax.experimental.pallas import tpu as pltpu
from jax.sharding import PartitionSpec as P

ORB = 12
NB = 8
SMAX = 32
REACH = 2
KPTS = 16
PAIR = ORB * ORB
LANES = 128
SPAN = 2 * REACH + 1
MESH = pl.DeviceIdType.MESH
BF = jnp.bfloat16
F32 = jnp.float32


def place():
    e = lax.axis_index("energy")
    m = lax.axis_index("momentum")
    return e // 2, e % 2, m // 2, m % 2


def partner(t, u):
    _, zl, zh, core = place()
    far = 1 - t // 2
    flip = ((t + 1) // 2) % 2
    zh_t = zh + far * (1 - 2 * zh)
    core_t = core + flip * (1 - 2 * core)
    zl_t = zl + u * (1 - 2 * zl)
    return zh_t * 2 + core_t, zl_t


def share(chunk, m, zl):
    if chunk == 0:
        return m + 4 * (m // 2), zl
    return m + 2, zl


def exchange_kernel(
    green, near_hbm, offsets_hbm, emit_hbm, absorb_hbm, coupling_hbm,
    out,
    arrived, made, left, right, left_out, right_out, outer, inner,
    base, t_main, t_left, t_right, pack, k_outer, k_inner,
    near, offsets, emit, absorb, coupling, ups,
    in_send, in_recv, in_local, x_send, x_recv, out_send, out_recv, out_local, y_send, y_recv, small,
):
    x, zl, zh, core = place()
    m = zh * 2 + core
    y = lax.axis_index("atom")

    def at(m_to, zl_to):
        return {"energy": x * 2 + zl_to, "momentum": m_to}

    x_left = {"energy": ((x + 3) % 4) * 2 + zl}
    x_right = {"energy": ((x + 1) % 4) * 2 + zl}
    y_left = {"atom": (y + 3) % 4}
    y_right = {"atom": (y + 1) % 4}

    barrier = pltpu.get_barrier_semaphore()
    steps = [(t, u) for t in range(4) for u in range(2) if (t, u) != (3, 0)]
    for t, u in steps:
        m_to, zl_to = partner(t, u)
        pl.semaphore_signal(barrier, inc=1, device_id=at(m_to, zl_to), device_id_type=MESH)
    for side in (x_left, x_right, y_left, y_right):
        pl.semaphore_signal(barrier, inc=1, device_id=side, device_id_type=MESH)
    fetches = [
        pltpu.make_async_copy(src, dst, small.at[i])
        for i, (src, dst) in enumerate(
            ((near_hbm, near), (offsets_hbm, offsets), (emit_hbm, emit), (absorb_hbm, absorb), (coupling_hbm, coupling))
        )
    ]
    for copy in fetches:
        copy.start()
    pl.semaphore_wait(barrier, len(steps) + 4)

    def rows(block, count=PAIR):
        return pl.ds(pl.multiple_of(block * count, 16), count)

    def send_in(chunk, t, u):
        m_to, zl_to = partner(t, u)
        atom, c = share(chunk, m_to, zl_to)
        return pltpu.make_async_remote_copy(
            src_ref=green.at[:, atom, c],
            dst_ref=arrived.at[chunk, pl.ds(m * 4, 4), rows(zl), :],
            send_sem=in_send.at[chunk, t, u],
            recv_sem=in_recv.at[chunk, t, u],
            device_id=at(m_to, zl_to),
            device_id_type=MESH,
        )

    def own_in(chunk):
        atom, c = share(chunk, m, zl)
        return pltpu.make_async_copy(
            green.at[:, atom, c], arrived.at[chunk, pl.ds(m * 4, 4), rows(zl), :], in_local.at[chunk]
        )

    for chunk in range(2):
        for t, u in steps:
            send_in(chunk, t, u).start()
        own_in(chunk).start()
    for copy in fetches:
        copy.wait()

    lane = lax.broadcasted_iota(jnp.int32, (KPTS, 2 * LANES), 1)
    line = lax.broadcasted_iota(jnp.int32, (KPTS, 2 * LANES), 0)
    shift = jnp.zeros((KPTS, 2 * LANES), jnp.int32)
    for w in range(KPTS):
        shift = jnp.where(line == w, offsets[w], shift)
    emit_pick = (lane == shift).astype(BF)
    absorb_pick = (lane == 2 * LANES - shift).astype(BF)
    dims = (((0,), (0,)), ((), ()))
    base[...] = lax.dot_general(emit[...], emit_pick, dims, preferred_element_type=F32) + lax.dot_general(
        absorb[...], absorb_pick, dims, preferred_element_type=F32
    )
    span = LANES + 2 * SMAX

    @pl.loop(0, KPTS)
    def _(lag):
        row = jnp.broadcast_to(base[pl.ds(lag, 1), :], (span, 2 * LANES))
        block = pltpu.roll(row, 2 * LANES - SMAX, 1, stride=1, stride_axis=0)[:, :LANES].astype(BF)
        for half in range(2):
            r = (2 * KPTS + half - lag) % KPTS
            for again in range(2):
                slot = r + KPTS * again
                cols = pl.ds(half * LANES, LANES)
                t_left[rows(slot, SMAX), cols] = block[:SMAX]
                t_main[rows(slot, LANES), cols] = block[SMAX : SMAX + LANES]
                t_right[rows(slot, SMAX), cols] = block[SMAX + LANES :]

    src = lax.broadcasted_iota(jnp.int32, (4 * LANES, 2 * LANES), 0)
    dst = lax.broadcasted_iota(jnp.int32, (4 * LANES, 2 * LANES), 1)
    within = dst % LANES
    wanted = (within // SMAX) * LANES + within % SMAX + (dst // LANES) * (LANES - SMAX)
    pack[...] = (src == wanted).astype(BF)

    prow = lax.broadcasted_iota(jnp.int32, (PAIR, ORB * NB), 0)
    pcol = lax.broadcasted_iota(jnp.int32, (PAIR, ORB * NB), 1)
    for n in range(NB):
        ups[n, 0] = ((prow // ORB) * NB + n == pcol).astype(BF)
        ups[n, 1] = ((prow % ORB) * NB + n == pcol).astype(BF)
    qrow = lax.broadcasted_iota(jnp.int32, (ORB, PAIR), 0)
    qcol = lax.broadcasted_iota(jnp.int32, (ORB, PAIR), 1)
    across_major = (qcol // ORB == qrow).astype(BF)
    across_minor = (qcol % ORB == qrow).astype(BF)

    @pl.loop(0, 8)
    def _(a):
        products = []
        steps_to = []
        blocks = coupling[a].reshape(ORB * NB, ORB)
        wide_major = jnp.dot(blocks, across_major, preferred_element_type=F32).astype(BF)
        wide_minor = jnp.dot(blocks, across_minor, preferred_element_type=F32).astype(BF)
        for n in range(NB):
            first = jnp.dot(ups[n, 0], wide_major, preferred_element_type=F32)
            second = jnp.dot(ups[n, 1], wide_minor, preferred_element_type=F32)
            products.append(first * second)
            steps_to.append(near[a, n] - y * 8 + REACH)
        for table, first_atom in ((k_outer, 8 * (a // 4)), (k_inner, 4)):
            parts = []
            for w in range(4):
                total = jnp.zeros((PAIR, PAIR), F32)
                for n in range(NB):
                    total = total + products[n] * (steps_to[n] == first_atom + w).astype(F32)
                parts.append(total)
            table[rows(a), :] = jnp.concatenate(parts, axis=1).astype(BF)

    keep_left = (x > 0).astype(F32)
    keep_right = (x < 3).astype(F32)

    def edge_copies(chunk):
        to_left = pltpu.make_async_remote_copy(
            src_ref=left_out.at[chunk], dst_ref=right.at[chunk, :, pl.ds(PAIR, PAIR), :],
            send_sem=x_send.at[chunk, 0], recv_sem=x_recv.at[chunk, 0],
            device_id=x_left, device_id_type=MESH,
        )
        to_right = pltpu.make_async_remote_copy(
            src_ref=right_out.at[chunk], dst_ref=left.at[chunk, :, pl.ds(0, PAIR), :],
            send_sem=x_send.at[chunk, 1], recv_sem=x_recv.at[chunk, 1],
            device_id=x_right, device_id_type=MESH,
        )
        return to_left, to_right

    def home(chunk, half):
        ks = pl.ds(2 * half, 2)
        return outer.at[ks, zl, m + REACH] if chunk == 0 else inner.at[ks, zl, m]

    def send_out(chunk, half, t, u):
        m_to, zl_to = partner(t, u)
        return pltpu.make_async_remote_copy(
            src_ref=made.at[chunk, pl.ds(m_to * 4 + 2 * half, 2), rows(zl_to), :],
            dst_ref=home(chunk, half),
            send_sem=out_send.at[chunk, half, t, u],
            recv_sem=out_recv.at[chunk, half, t, u],
            device_id=at(m_to, zl_to),
            device_id_type=MESH,
        )

    def own_out(chunk, half):
        return pltpu.make_async_copy(
            made.at[chunk, pl.ds(m * 4 + 2 * half, 2), rows(zl), :], home(chunk, half), out_local.at[chunk, half]
        )

    for chunk in range(2):
        for t, u in steps:
            send_in(chunk, t, u).wait_recv()
        own_in(chunk).wait()

        for group in range(4):
            four = jnp.concatenate([arrived[chunk, group * 4 + i] for i in range(4)], axis=1)
            packed = jnp.dot(four, pack[...], preferred_element_type=F32)
            left_out[chunk, group] = (packed[:PAIR, :LANES] * keep_left).astype(BF)
            left[chunk, group, PAIR:, :] = packed[:PAIR, LANES:].astype(BF)
            right[chunk, group, :PAIR, :] = packed[PAIR:, :LANES].astype(BF)
            right_out[chunk, group] = (packed[PAIR:, LANES:] * keep_right).astype(BF)
        edges = edge_copies(chunk)
        for copy in edges:
            copy.start()
        for copy in edges:
            copy.wait()

        @pl.loop(0, 8)
        def _(turn):
            half, t = turn // 4, turn % 4
            m_to, _ = partner(t, 0)
            kp = m_to * 2 + half
            start = KPTS - 2 * kp
            main = jnp.concatenate([arrived[chunk, q] for q in range(KPTS)], axis=1)
            total = jnp.dot(
                main, t_main[pl.ds(pl.multiple_of(start * LANES, LANES), KPTS * LANES), :],
                preferred_element_type=F32,
            )
            window = pl.ds(pl.multiple_of(start * SMAX, SMAX), KPTS * SMAX)
            lows = jnp.concatenate([left[chunk, g] for g in range(4)], axis=1)
            total = total + jnp.dot(lows, t_left[window, :], preferred_element_type=F32)
            highs = jnp.concatenate([right[chunk, g] for g in range(4)], axis=1)
            total = total + jnp.dot(highs, t_right[window, :], preferred_element_type=F32)
            total = total.astype(BF)
            made[chunk, 2 * kp] = total[:, :LANES]
            made[chunk, 2 * kp + 1] = total[:, LANES:]
            send_out(chunk, half, t, 1).start()

            @pl.when(t < 3)
            def _():
                send_out(chunk, half, t, 0).start()

            @pl.when(t == 3)
            def _():
                own_out(chunk, half).start()

    def landed(chunk, half):
        for t, u in steps:
            send_out(chunk, half, t, u).wait_recv()
        own_out(chunk, half).wait()

    def y_copies(half):
        ks = pl.ds(2 * half, 2)
        down = pltpu.make_async_remote_copy(
            src_ref=outer.at[ks, :, pl.ds(2, 2)], dst_ref=outer.at[ks, :, pl.ds(6, 2)],
            send_sem=y_send.at[half, 0], recv_sem=y_recv.at[half, 0], device_id=y_left, device_id_type=MESH,
        )
        up = pltpu.make_async_remote_copy(
            src_ref=outer.at[ks, :, pl.ds(4, 2)], dst_ref=outer.at[ks, :, pl.ds(0, 2)],
            send_sem=y_send.at[half, 1], recv_sem=y_recv.at[half, 1], device_id=y_right, device_id_type=MESH,
        )
        return down, up

    def pair_of(source, half, c, first):
        two = [source[2 * half + j, c, pl.ds(first, 4)].reshape(4 * PAIR, LANES) for j in range(2)]
        return jnp.concatenate(two, axis=1)

    def apply_outer(half):
        @pl.loop(0, 4)
        def _(turn):
            c, side = turn // 2, turn % 2
            operand = pair_of(outer, half, c, 4 * side)
            for part in range(2):
                a = 4 * side + 2 * part
                block = jnp.dot(k_outer[rows(2 * side + part, 2 * PAIR), :], operand, preferred_element_type=F32)
                for i in range(2):
                    for j in range(2):
                        out[2 * half + j, a + i, c] = block[i * PAIR : (i + 1) * PAIR, j * LANES : (j + 1) * LANES]

    def apply_inner(half):
        @pl.loop(0, 4)
        def _(turn):
            c, side = turn // 2, turn % 2
            operand = pair_of(inner, half, c, 0)
            for part in range(2):
                a = 4 * side + 2 * part
                block = jnp.dot(k_inner[rows(2 * side + part, 2 * PAIR), :], operand, preferred_element_type=F32)
                for i in range(2):
                    for j in range(2):
                        out[2 * half + j, a + i, c] += block[i * PAIR : (i + 1) * PAIR, j * LANES : (j + 1) * LANES]

    for half in range(2):
        landed(0, half)
        for copy in y_copies(half):
            copy.start()
    for half in range(2):
        for copy in y_copies(half):
            copy.wait()
        apply_outer(half)
    for chunk in range(2):
        for t, u in steps:
            send_in(chunk, t, u).wait_send()
    for half in range(2):
        landed(1, half)
        apply_inner(half)
    for chunk in range(2):
        for half in range(2):
            for t, u in steps:
                send_out(chunk, half, t, u).wait_send()


def shards(green, neighbours, offsets, emit_weight, absorb_weight, coupling):
    k_count, a_count, components, e_count = green.shape
    hbm = pl.BlockSpec(memory_space=pltpu.HBM)
    dma = pltpu.SemaphoreType.DMA
    vmem = pltpu.VMEM
    out = pl.pallas_call(
        exchange_kernel,
        out_shape=jax.ShapeDtypeStruct((k_count, a_count, 2, PAIR, e_count), F32),
        in_specs=[hbm] * 6,
        out_specs=pl.BlockSpec(memory_space=pltpu.VMEM),
        scratch_shapes=[
            vmem((2, KPTS, 2 * PAIR, LANES), BF),
            vmem((2, KPTS, 2 * PAIR, LANES), BF),
            vmem((2, 4, 2 * PAIR, LANES), BF),
            vmem((2, 4, 2 * PAIR, LANES), BF),
            vmem((2, 4, PAIR, LANES), BF),
            vmem((2, 4, PAIR, LANES), BF),
            vmem((k_count, 2, 8, PAIR, LANES), BF),
            vmem((k_count, 2, 4, PAIR, LANES), BF),
            vmem((KPTS, 2 * LANES), F32),
            vmem((2 * KPTS * LANES, 2 * LANES), BF),
            vmem((2 * KPTS * SMAX, 2 * LANES), BF),
            vmem((2 * KPTS * SMAX, 2 * LANES), BF),
            vmem((4 * LANES, 2 * LANES), BF),
            vmem((a_count * PAIR, 4 * PAIR), BF),
            vmem((a_count * PAIR, 4 * PAIR), BF),
            pltpu.SMEM((a_count, NB), jnp.int32),
            pltpu.SMEM((KPTS,), jnp.int32),
            vmem((KPTS, KPTS), BF),
            vmem((KPTS, KPTS), BF),
            vmem((a_count, ORB, NB, ORB), BF),
            vmem((NB, 2, PAIR, ORB * NB), BF),
            dma((2, 4, 2)), dma((2, 4, 2)), dma((2,)),
            dma((2, 2)), dma((2, 2)),
            dma((2, 2, 4, 2)), dma((2, 2, 4, 2)), dma((2, 2)),
            dma((2, 2)), dma((2, 2)), dma((5,)),
        ],
        compiler_params=pltpu.CompilerParams(
            collective_id=0, has_side_effects=True, vmem_limit_bytes=40 * 1024 * 1024
        ),
        name="exchange",
    )(
        *(
            pltpu.with_memory_space_constraint(array, pltpu.HBM)
            for array in (
                green.reshape(k_count, a_count, 2, PAIR, e_count),
                neighbours,
                offsets,
                emit_weight,
                absorb_weight,
                coupling.transpose(0, 2, 1, 3),
            )
        )
    )
    return out.reshape(k_count, a_count, components, e_count)


def solution(mesh):
    in_specs = (
        P("momentum", "atom", None, "energy"),
        P("atom", None),
        P(),
        P(),
        P(),
        P("atom", None, None, None),
    )
    out_specs = P("momentum", "atom", None, "energy")
    return jax.shard_map(shards, mesh=mesh, in_specs=in_specs, out_specs=out_specs, check_vma=False)
```

time: 81.3 us -> 70 us (0.86)
  Pallas kernels: 73.5 us -> 67.7 us
  local copies, waits for them, and re-layouts: 7.42 us -> 2.19 us
    pallas_call x2 -> x1, Pallas kernels: 73.5 us -> 67.7 us  [shards(): pl.pallas_call(exchange_kernel, out_shape=jax.ShapeDtypeStruct((k_count,...]
    unnamed x11 -> x1, local copies, waits for them, and re-layouts: 6.69 us -> 2.19 us
where the time goes in v2:
time: 70 us; the launch traced here: 69.9 us
  Pallas kernels  67.7 us (97%)
  local copies, waits for them, and re-layouts  2.19 us (3%)
    pallas_call x1, Pallas kernels, shards(): pl.pallas_call(exchange_kernel, out_shape=jax.ShapeDtypeStruct((k_count,...  67.7 us
    unnamed x1, local copies, waits for them, and re-layouts  2.19 us

profile of v2, /device:TPU:1, one launch (start us, length us, event | category | flops | bytes accessed | tf_op | source)
XLA Modules:
  0.0 69.9 jit_solution(4155726642235821963)
XLA Ops:
  0.0 67.7 %exchange.1 = f32[4,8,2,144,128]{4,3,2,1,0:T(8,128)S(1)} custom-call(bf16[4,8,2,144,128]{4,3,2,1,0:T(8,128)(2,1)} %bitcast.4, s32[8,8]{1,0:T(8,128)} %near_hbm.1, s32[16]{0:T(128)} %offsets_hbm.1, bf16[16,16]{1,0:T(8,128)(2,1)} %emit_hbm.1, bf16[16,16]{1,0:T(8,128)(2,1)} %absorb_hbm.1, bf16[8,12,8,12]{3,2,1,0:T(8,128)(2,1)} %bitcast.5), custom_call_target="tpu_custom_call" | custom-call | tf_op jit(solution)/shard_map/exchange/pallas_call | solution.py:326
  67.7 2.2 %copy.8 = f32[4,8,288,128]{3,2,1,0:T(8,128)} copy(f32[4,8,288,128]{3,2,1,0:T(8,128)S(1)} %bitcast.3) | data formatting | bytes 9437184

commit v3 on v2

--- a/solution.py
+++ b/solution.py
@@ -173,15 +173,16 @@
     keep_left = (x > 0).astype(F32)
     keep_right = (x < 3).astype(F32)
 
-    def edge_copies(chunk):
+    def edge_copies(chunk, t):
+        group, _ = partner(t, 0)
         to_left = pltpu.make_async_remote_copy(
-            src_ref=left_out.at[chunk], dst_ref=right.at[chunk, :, pl.ds(PAIR, PAIR), :],
-            send_sem=x_send.at[chunk, 0], recv_sem=x_recv.at[chunk, 0],
+            src_ref=left_out.at[chunk, group], dst_ref=right.at[chunk, group, pl.ds(PAIR, PAIR), :],
+            send_sem=x_send.at[chunk, t, 0], recv_sem=x_recv.at[chunk, t, 0],
             device_id=x_left, device_id_type=MESH,
         )
         to_right = pltpu.make_async_remote_copy(
-            src_ref=right_out.at[chunk], dst_ref=left.at[chunk, :, pl.ds(0, PAIR), :],
-            send_sem=x_send.at[chunk, 1], recv_sem=x_recv.at[chunk, 1],
+            src_ref=right_out.at[chunk, group], dst_ref=left.at[chunk, group, pl.ds(0, PAIR), :],
+            send_sem=x_send.at[chunk, t, 1], recv_sem=x_recv.at[chunk, t, 1],
             device_id=x_right, device_id_type=MESH,
         )
         return to_left, to_right
@@ -206,23 +207,47 @@
             made.at[chunk, pl.ds(m * 4 + 2 * half, 2), rows(zl), :], home(chunk, half), out_local.at[chunk, half]
         )
 
+    def landed(chunk, half):
+        for t, u in steps:
+            send_out(chunk, half, t, u).wait_recv()
+        own_out(chunk, half).wait()
+
+    def y_copies(half):
+        ks = pl.ds(2 * half, 2)
+        down = pltpu.make_async_remote_copy(
+            src_ref=outer.at[ks, :, pl.ds(2, 2)], dst_ref=outer.at[ks, :, pl.ds(6, 2)],
+            send_sem=y_send.at[half, 0], recv_sem=y_recv.at[half, 0], device_id=y_left, device_id_type=MESH,
+        )
+        up = pltpu.make_async_remote_copy(
+            src_ref=outer.at[ks, :, pl.ds(4, 2)], dst_ref=outer.at[ks, :, pl.ds(0, 2)],
+            send_sem=y_send.at[half, 1], recv_sem=y_recv.at[half, 1], device_id=y_right, device_id_type=MESH,
+        )
+        return down, up
+
+    def spread(half):
+        landed(0, half)
+        for copy in y_copies(half):
+            copy.start()
+
     for chunk in range(2):
-        for t, u in steps:
-            send_in(chunk, t, u).wait_recv()
-        own_in(chunk).wait()
-
-        for group in range(4):
+        for t in range(4):
+            if t < 3:
+                send_in(chunk, t, 0).wait_recv()
+            else:
+                own_in(chunk).wait()
+            send_in(chunk, t, 1).wait_recv()
+            group, _ = partner(t, 0)
             four = jnp.concatenate([arrived[chunk, group * 4 + i] for i in range(4)], axis=1)
             packed = jnp.dot(four, pack[...], preferred_element_type=F32)
             left_out[chunk, group] = (packed[:PAIR, :LANES] * keep_left).astype(BF)
             left[chunk, group, PAIR:, :] = packed[:PAIR, LANES:].astype(BF)
             right[chunk, group, :PAIR, :] = packed[PAIR:, :LANES].astype(BF)
             right_out[chunk, group] = (packed[PAIR:, LANES:] * keep_right).astype(BF)
-        edges = edge_copies(chunk)
-        for copy in edges:
-            copy.start()
-        for copy in edges:
-            copy.wait()
+            for copy in edge_copies(chunk, t):
+                copy.start()
+        for t in range(4):
+            for copy in edge_copies(chunk, t):
+                copy.wait()
 
         @pl.loop(0, 8)
         def _(turn):
@@ -244,8 +269,9 @@
             made[chunk, 2 * kp] = total[:, :LANES]
             made[chunk, 2 * kp + 1] = total[:, LANES:]
             send_out(chunk, half, t, 1).start()
-
-            @pl.when(t < 3)
+            straight = turn < 4 if chunk == 1 else turn < 8
+
+            @pl.when(straight & (t < 3))
             def _():
                 send_out(chunk, half, t, 0).start()
 
@@ -253,22 +279,15 @@
             def _():
                 own_out(chunk, half).start()
 
-    def landed(chunk, half):
-        for t, u in steps:
-            send_out(chunk, half, t, u).wait_recv()
-        own_out(chunk, half).wait()
-
-    def y_copies(half):
-        ks = pl.ds(2 * half, 2)
-        down = pltpu.make_async_remote_copy(
-            src_ref=outer.at[ks, :, pl.ds(2, 2)], dst_ref=outer.at[ks, :, pl.ds(6, 2)],
-            send_sem=y_send.at[half, 0], recv_sem=y_recv.at[half, 0], device_id=y_left, device_id_type=MESH,
-        )
-        up = pltpu.make_async_remote_copy(
-            src_ref=outer.at[ks, :, pl.ds(4, 2)], dst_ref=outer.at[ks, :, pl.ds(0, 2)],
-            send_sem=y_send.at[half, 1], recv_sem=y_recv.at[half, 1], device_id=y_right, device_id_type=MESH,
-        )
-        return down, up
+            if chunk == 1:
+
+                @pl.when(turn == 1)
+                def _():
+                    spread(0)
+
+    for t in range(3):
+        send_out(1, 1, t, 0).start()
+    spread(1)
 
     def pair_of(source, half, c, first):
         two = [source[2 * half + j, c, pl.ds(first, 4)].reshape(4 * PAIR, LANES) for j in range(2)]
@@ -286,10 +305,9 @@
                     for j in range(2):
                         out[2 * half + j, a + i, c] = block[i * PAIR : (i + 1) * PAIR, j * LANES : (j + 1) * LANES]
 
-    def apply_inner(half):
-        @pl.loop(0, 4)
-        def _(turn):
-            c, side = turn // 2, turn % 2
+    def apply_inner(half, c):
+        @pl.loop(0, 2)
+        def _(side):
             operand = pair_of(inner, half, c, 0)
             for part in range(2):
                 a = 4 * side + 2 * part
@@ -299,19 +317,19 @@
                         out[2 * half + j, a + i, c] += block[i * PAIR : (i + 1) * PAIR, j * LANES : (j + 1) * LANES]
 
     for half in range(2):
-        landed(0, half)
-        for copy in y_copies(half):
-            copy.start()
-    for half in range(2):
         for copy in y_copies(half):
             copy.wait()
         apply_outer(half)
+        for t in range(4):
+            send_out(1, half, t, 1).wait_recv()
+        apply_inner(half, 1 - zl)
+        for t in range(3):
+            send_out(1, half, t, 0).wait_recv()
+        own_out(1, half).wait()
+        apply_inner(half, zl)
     for chunk in range(2):
         for t, u in steps:
             send_in(chunk, t, u).wait_send()
-    for half in range(2):
-        landed(1, half)
-        apply_inner(half)
     for chunk in range(2):
         for half in range(2):
             for t, u in steps:
@@ -351,7 +369,7 @@
             vmem((a_count, ORB, NB, ORB), BF),
             vmem((NB, 2, PAIR, ORB * NB), BF),
             dma((2, 4, 2)), dma((2, 4, 2)), dma((2,)),
-            dma((2, 2)), dma((2, 2)),
+            dma((2, 4, 2)), dma((2, 4, 2)),
             dma((2, 2, 4, 2)), dma((2, 2, 4, 2)), dma((2, 2)),
             dma((2, 2)), dma((2, 2)), dma((5,)),
         ],

time: 70 us -> 64.9 us (0.927)
  Pallas kernels: 67.7 us -> 62.6 us
    pallas_call x1, Pallas kernels: 67.7 us -> 62.6 us  [shards(): pl.pallas_call(exchange_kernel, out_shape=jax.ShapeDtypeStruct((k_count,...]
where the time goes in v3:
time: 64.9 us; the launch traced here: 64.8 us
  Pallas kernels  62.6 us (96%)
  local copies, waits for them, and re-layouts  2.19 us (3%)
    pallas_call x1, Pallas kernels, shards(): pl.pallas_call(exchange_kernel, out_shape=jax.ShapeDtypeStruct((k_count,...  62.6 us
    unnamed x1, local copies, waits for them, and re-layouts  2.19 us

profile of v3, /device:TPU:1, one launch (start us, length us, event | category | flops | bytes accessed | tf_op | source)
XLA Modules:
  0.0 64.8 jit_solution(8282623142971653712)
XLA Ops:
  0.0 62.6 %exchange.1 = f32[4,8,2,144,128]{4,3,2,1,0:T(8,128)S(1)} custom-call(bf16[4,8,2,144,128]{4,3,2,1,0:T(8,128)(2,1)} %bitcast.4, s32[8,8]{1,0:T(8,128)} %near_hbm.1, s32[16]{0:T(128)} %offsets_hbm.1, bf16[16,16]{1,0:T(8,128)(2,1)} %emit_hbm.1, bf16[16,16]{1,0:T(8,128)(2,1)} %absorb_hbm.1, bf16[8,12,8,12]{3,2,1,0:T(8,128)(2,1)} %bitcast.5), custom_call_target="tpu_custom_call" | custom-call | tf_op jit(solution)/shard_map/exchange/pallas_call | solution.py:344
  62.6 2.2 %copy.8 = f32[4,8,288,128]{3,2,1,0:T(8,128)} copy(f32[4,8,288,128]{3,2,1,0:T(8,128)S(1)} %bitcast.3) | data formatting | bytes 9437184

commit v4 on v3

--- a/solution.py
+++ b/solution.py
@@ -49,6 +49,7 @@
     base, t_main, t_left, t_right, pack, k_outer, k_inner,
     near, offsets, emit, absorb, coupling, ups,
     in_send, in_recv, in_local, x_send, x_recv, out_send, out_recv, out_local, y_send, y_recv, small,
+    sides_in, told,
 ):
     x, zl, zh, core = place()
     m = zh * 2 + core
@@ -64,11 +65,17 @@
 
     barrier = pltpu.get_barrier_semaphore()
     steps = [(t, u) for t in range(4) for u in range(2) if (t, u) != (3, 0)]
+    sides = (x_left, x_right, y_left, y_right)
+    head = m * 2 + zl == 0
     for t, u in steps:
         m_to, zl_to = partner(t, u)
         pl.semaphore_signal(barrier, inc=1, device_id=at(m_to, zl_to), device_id_type=MESH)
-    for side in (x_left, x_right, y_left, y_right):
-        pl.semaphore_signal(barrier, inc=1, device_id=side, device_id_type=MESH)
+
+    @pl.when(head)
+    def _():
+        for side in sides:
+            pl.semaphore_signal(barrier, inc=1, device_id=side, device_id_type=MESH)
+
     fetches = [
         pltpu.make_async_copy(src, dst, small.at[i])
         for i, (src, dst) in enumerate(
@@ -77,7 +84,8 @@
     ]
     for copy in fetches:
         copy.start()
-    pl.semaphore_wait(barrier, len(steps) + 4)
+    pl.semaphore_wait(barrier, len(steps) + len(sides) * head.astype(jnp.int32))
+
 
     def rows(block, count=PAIR):
         return pl.ds(pl.multiple_of(block * count, 16), count)
@@ -170,6 +178,19 @@
                 parts.append(total)
             table[rows(a), :] = jnp.concatenate(parts, axis=1).astype(BF)
 
+    @pl.when(head)
+    def _():
+        for side in sides:
+            pl.semaphore_signal(sides_in, inc=1, device_id=side, device_id_type=MESH)
+        pl.semaphore_wait(sides_in, len(sides))
+        for t, u in steps:
+            m_to, zl_to = partner(t, u)
+            pl.semaphore_signal(told, inc=1, device_id=at(m_to, zl_to), device_id_type=MESH)
+
+    @pl.when(jnp.logical_not(head))
+    def _():
+        pl.semaphore_wait(told, 1)
+
     keep_left = (x > 0).astype(F32)
     keep_right = (x < 3).astype(F32)
 
@@ -207,26 +228,35 @@
             made.at[chunk, pl.ds(m * 4 + 2 * half, 2), rows(zl), :], home(chunk, half), out_local.at[chunk, half]
         )
 
-    def landed(chunk, half):
-        for t, u in steps:
-            send_out(chunk, half, t, u).wait_recv()
-        own_out(chunk, half).wait()
-
-    def y_copies(half):
-        ks = pl.ds(2 * half, 2)
+    def landed(chunk, half, part):
+        if part == 0:
+            for t in range(4):
+                send_out(chunk, half, t, 1).wait_recv()
+        else:
+            for t in range(3):
+                send_out(chunk, half, t, 0).wait_recv()
+            own_out(chunk, half).wait()
+
+    def c_of(part):
+        return zl if part else 1 - zl
+
+    def y_copies(half, part):
+        ks, c = pl.ds(2 * half, 2), c_of(part)
         down = pltpu.make_async_remote_copy(
-            src_ref=outer.at[ks, :, pl.ds(2, 2)], dst_ref=outer.at[ks, :, pl.ds(6, 2)],
-            send_sem=y_send.at[half, 0], recv_sem=y_recv.at[half, 0], device_id=y_left, device_id_type=MESH,
+            src_ref=outer.at[ks, c, pl.ds(2, 2)], dst_ref=outer.at[ks, c, pl.ds(6, 2)],
+            send_sem=y_send.at[half, part, 0], recv_sem=y_recv.at[half, part, 0],
+            device_id=y_left, device_id_type=MESH,
         )
         up = pltpu.make_async_remote_copy(
-            src_ref=outer.at[ks, :, pl.ds(4, 2)], dst_ref=outer.at[ks, :, pl.ds(0, 2)],
-            send_sem=y_send.at[half, 1], recv_sem=y_recv.at[half, 1], device_id=y_right, device_id_type=MESH,
+            src_ref=outer.at[ks, c, pl.ds(4, 2)], dst_ref=outer.at[ks, c, pl.ds(0, 2)],
+            send_sem=y_send.at[half, part, 1], recv_sem=y_recv.at[half, part, 1],
+            device_id=y_right, device_id_type=MESH,
         )
         return down, up
 
-    def spread(half):
-        landed(0, half)
-        for copy in y_copies(half):
+    def spread(half, part):
+        landed(0, half, part)
+        for copy in y_copies(half, part):
             copy.start()
 
     for chunk in range(2):
@@ -245,6 +275,8 @@
             right_out[chunk, group] = (packed[PAIR:, LANES:] * keep_right).astype(BF)
             for copy in edge_copies(chunk, t):
                 copy.start()
+        if chunk == 1:
+            spread(0, 0)
         for t in range(4):
             for copy in edge_copies(chunk, t):
                 copy.wait()
@@ -269,34 +301,36 @@
             made[chunk, 2 * kp] = total[:, :LANES]
             made[chunk, 2 * kp + 1] = total[:, LANES:]
             send_out(chunk, half, t, 1).start()
-            straight = turn < 4 if chunk == 1 else turn < 8
-
-            @pl.when(straight & (t < 3))
-            def _():
-                send_out(chunk, half, t, 0).start()
 
             @pl.when(t == 3)
             def _():
+                for near_t in range(3):
+                    send_out(chunk, half, near_t, 0).start()
                 own_out(chunk, half).start()
 
             if chunk == 1:
 
-                @pl.when(turn == 1)
+                @pl.when(turn == 0)
                 def _():
-                    spread(0)
-
-    for t in range(3):
-        send_out(1, 1, t, 0).start()
-    spread(1)
+                    spread(0, 1)
+
+                @pl.when(turn == 5)
+                def _():
+                    spread(1, 0)
+
+    spread(1, 1)
 
     def pair_of(source, half, c, first):
         two = [source[2 * half + j, c, pl.ds(first, 4)].reshape(4 * PAIR, LANES) for j in range(2)]
         return jnp.concatenate(two, axis=1)
 
-    def apply_outer(half):
-        @pl.loop(0, 4)
-        def _(turn):
-            c, side = turn // 2, turn % 2
+    def apply_outer(half, part):
+        for copy in y_copies(half, part):
+            copy.wait()
+        c = c_of(part)
+
+        @pl.loop(0, 2)
+        def _(side):
             operand = pair_of(outer, half, c, 4 * side)
             for part in range(2):
                 a = 4 * side + 2 * part
@@ -305,7 +339,10 @@
                     for j in range(2):
                         out[2 * half + j, a + i, c] = block[i * PAIR : (i + 1) * PAIR, j * LANES : (j + 1) * LANES]
 
-    def apply_inner(half, c):
+    def apply_inner(half, part):
+        landed(1, half, part)
+        c = c_of(part)
+
         @pl.loop(0, 2)
         def _(side):
             operand = pair_of(inner, half, c, 0)
@@ -316,17 +353,14 @@
                     for j in range(2):
                         out[2 * half + j, a + i, c] += block[i * PAIR : (i + 1) * PAIR, j * LANES : (j + 1) * LANES]
 
-    for half in range(2):
-        for copy in y_copies(half):
-            copy.wait()
-        apply_outer(half)
-        for t in range(4):
-            send_out(1, half, t, 1).wait_recv()
-        apply_inner(half, 1 - zl)
-        for t in range(3):
-            send_out(1, half, t, 0).wait_recv()
-        own_out(1, half).wait()
-        apply_inner(half, zl)
+    apply_outer(0, 0)
+    apply_outer(0, 1)
+    apply_inner(0, 0)
+    apply_outer(1, 0)
+    apply_inner(0, 1)
+    apply_outer(1, 1)
+    apply_inner(1, 0)
+    apply_inner(1, 1)
     for chunk in range(2):
         for t, u in steps:
             send_in(chunk, t, u).wait_send()
@@ -340,6 +374,7 @@
     k_count, a_count, components, e_count = green.shape
     hbm = pl.BlockSpec(memory_space=pltpu.HBM)
     dma = pltpu.SemaphoreType.DMA
+    regular = pltpu.SemaphoreType.REGULAR
     vmem = pltpu.VMEM
     out = pl.pallas_call(
         exchange_kernel,
@@ -371,7 +406,8 @@
             dma((2, 4, 2)), dma((2, 4, 2)), dma((2,)),
             dma((2, 4, 2)), dma((2, 4, 2)),
             dma((2, 2, 4, 2)), dma((2, 2, 4, 2)), dma((2, 2)),
-            dma((2, 2)), dma((2, 2)), dma((5,)),
+            dma((2, 2, 2)), dma((2, 2, 2)), dma((5,)),
+            regular, regular,
         ],
         compiler_params=pltpu.CompilerParams(
             collective_id=0, has_side_effects=True, vmem_limit_bytes=40 * 1024 * 1024

time: 64.9 us -> 62.8 us (0.968)
  Pallas kernels: 62.6 us -> 60.5 us
    pallas_call x1, Pallas kernels: 62.6 us -> 60.5 us  [shards(): pl.pallas_call(exchange_kernel, out_shape=jax.ShapeDtypeStruct((k_count,...]
where the time goes in v4:
time: 62.8 us; the launch traced here: 62.7 us
  Pallas kernels  60.5 us (96%)
  local copies, waits for them, and re-layouts  2.19 us (3%)
    pallas_call x1, Pallas kernels, shards(): pl.pallas_call(exchange_kernel, out_shape=jax.ShapeDtypeStruct((k_count,...  60.5 us
    unnamed x1, local copies, waits for them, and re-layouts  2.19 us

profile of v4, /device:TPU:1, one launch (start us, length us, event | category | flops | bytes accessed | tf_op | source)
XLA Modules:
  0.0 62.7 jit_solution(9980514804637704694)
XLA Ops:
  0.0 60.5 %exchange.1 = f32[4,8,2,144,128]{4,3,2,1,0:T(8,128)S(1)} custom-call(bf16[4,8,2,144,128]{4,3,2,1,0:T(8,128)(2,1)} %bitcast.4, s32[8,8]{1,0:T(8,128)} %near_hbm.1, s32[16]{0:T(128)} %offsets_hbm.1, bf16[16,16]{1,0:T(8,128)(2,1)} %emit_hbm.1, bf16[16,16]{1,0:T(8,128)(2,1)} %absorb_hbm.1, bf16[8,12,8,12]{3,2,1,0:T(8,128)(2,1)} %bitcast.5), custom_call_target="tpu_custom_call" | custom-call | tf_op jit(solution)/shard_map/exchange/pallas_call | solution.py:379
  60.5 2.2 %copy.8 = f32[4,8,288,128]{3,2,1,0:T(8,128)} copy(f32[4,8,288,128]{3,2,1,0:T(8,128)S(1)} %bitcast.3) | data formatting | bytes 9437184

commit v5 on v4

--- a/solution.py
+++ b/solution.py
@@ -43,11 +43,11 @@
 
 
 def exchange_kernel(
-    green, near_hbm, offsets_hbm, emit_hbm, absorb_hbm, coupling_hbm,
-    out,
-    arrived, made, left, right, left_out, right_out, outer, inner,
-    base, t_main, t_left, t_right, pack, k_outer, k_inner,
-    near, offsets, emit, absorb, coupling, ups,
+    green_hbm, near_hbm, offsets_hbm, emit_hbm, absorb_hbm, coupling_hbm,
+    out, inner, k_inner,
+    arrived, made, left, right, left_out, right_out, outer,
+    base, t_main, t_left, t_right, pack, k_outer,
+    near, offsets, emit, absorb, coupling, ups, green,
     in_send, in_recv, in_local, x_send, x_recv, out_send, out_recv, out_local, y_send, y_recv, small,
     sides_in, told,
 ):
@@ -65,6 +65,8 @@
 
     barrier = pltpu.get_barrier_semaphore()
     steps = [(t, u) for t in range(4) for u in range(2) if (t, u) != (3, 0)]
+    prefetch = pltpu.make_async_copy(green_hbm, green, small.at[5])
+    prefetch.start()
     sides = (x_left, x_right, y_left, y_right)
     head = m * 2 + zl == 0
     for t, u in steps:
@@ -84,6 +86,7 @@
     ]
     for copy in fetches:
         copy.start()
+    prefetch.wait()
     pl.semaphore_wait(barrier, len(steps) + len(sides) * head.astype(jnp.int32))
 
 
@@ -229,7 +232,7 @@
         )
 
     def landed(chunk, half, part):
-        if part == 0:
+        if part == 1:
             for t in range(4):
                 send_out(chunk, half, t, 1).wait_recv()
         else:
@@ -238,7 +241,7 @@
             own_out(chunk, half).wait()
 
     def c_of(part):
-        return zl if part else 1 - zl
+        return 1 - zl if part else zl
 
     def y_copies(half, part):
         ks, c = pl.ds(2 * half, 2), c_of(part)
@@ -300,13 +303,16 @@
             total = total.astype(BF)
             made[chunk, 2 * kp] = total[:, :LANES]
             made[chunk, 2 * kp + 1] = total[:, LANES:]
-            send_out(chunk, half, t, 1).start()
+
+            @pl.when(t < 3)
+            def _():
+                send_out(chunk, half, t, 0).start()
 
             @pl.when(t == 3)
             def _():
-                for near_t in range(3):
-                    send_out(chunk, half, near_t, 0).start()
                 own_out(chunk, half).start()
+                for near_t in range(4):
+                    send_out(chunk, half, near_t, 1).start()
 
             if chunk == 1:
 
@@ -360,7 +366,7 @@
     apply_inner(0, 1)
     apply_outer(1, 1)
     apply_inner(1, 0)
-    apply_inner(1, 1)
+    landed(1, 1, 1)
     for chunk in range(2):
         for t, u in steps:
             send_in(chunk, t, u).wait_send()
@@ -370,17 +376,49 @@
                 send_out(chunk, half, t, u).wait_send()
 
 
+def finish_kernel(most, last, k_inner, out, block, sems):
+    c = 1 - lax.axis_index("energy") % 2
+    first = pl.ds(0, 2)
+    second = pl.ds(2, 2)
+    copies = [
+        pltpu.make_async_copy(most.at[first], out.at[first], sems.at[0]),
+        pltpu.make_async_copy(most.at[second, :, 1 - c], out.at[second, :, 1 - c], sems.at[1]),
+    ]
+    for copy in copies:
+        copy.start()
+    operand = jnp.concatenate([last[2 + j, c].reshape(4 * PAIR, LANES) for j in range(2)], axis=1)
+    for side in range(2):
+        for part in range(2):
+            a = 4 * side + 2 * part
+            product = jnp.dot(k_inner[a * PAIR : (a + 2) * PAIR, :], operand, preferred_element_type=F32)
+            for i in range(2):
+                for j in range(2):
+                    block[j, a + i] = most[2 + j, a + i, c] + product[i * PAIR : (i + 1) * PAIR, j * LANES : (j + 1) * LANES]
+        atoms = pl.ds(4 * side, 4)
+        copy = pltpu.make_async_copy(block.at[:, atoms], out.at[second, atoms, c], sems.at[2 + side])
+        copy.start()
+        copies.append(copy)
+    for copy in copies:
+        copy.wait()
+
+
 def shards(green, neighbours, offsets, emit_weight, absorb_weight, coupling):
     k_count, a_count, components, e_count = green.shape
     hbm = pl.BlockSpec(memory_space=pltpu.HBM)
     dma = pltpu.SemaphoreType.DMA
     regular = pltpu.SemaphoreType.REGULAR
     vmem = pltpu.VMEM
-    out = pl.pallas_call(
+    shape = jax.ShapeDtypeStruct((k_count, a_count, 2, PAIR, e_count), F32)
+    in_vmem = pl.BlockSpec(memory_space=vmem)
+    most, last, k_inner = pl.pallas_call(
         exchange_kernel,
-        out_shape=jax.ShapeDtypeStruct((k_count, a_count, 2, PAIR, e_count), F32),
+        out_shape=(
+            shape,
+            jax.ShapeDtypeStruct((k_count, 2, 4, PAIR, LANES), BF),
+            jax.ShapeDtypeStruct((a_count * PAIR, 4 * PAIR), BF),
+        ),
         in_specs=[hbm] * 6,
-        out_specs=pl.BlockSpec(memory_space=pltpu.VMEM),
+        out_specs=(in_vmem,) * 3,
         scratch_shapes=[
             vmem((2, KPTS, 2 * PAIR, LANES), BF),
             vmem((2, KPTS, 2 * PAIR, LANES), BF),
@@ -389,13 +427,11 @@
             vmem((2, 4, PAIR, LANES), BF),
             vmem((2, 4, PAIR, LANES), BF),
             vmem((k_count, 2, 8, PAIR, LANES), BF),
-            vmem((k_count, 2, 4, PAIR, LANES), BF),
             vmem((KPTS, 2 * LANES), F32),
             vmem((2 * KPTS * LANES, 2 * LANES), BF),
             vmem((2 * KPTS * SMAX, 2 * LANES), BF),
             vmem((2 * KPTS * SMAX, 2 * LANES), BF),
             vmem((4 * LANES, 2 * LANES), BF),
-            vmem((a_count * PAIR, 4 * PAIR), BF),
             vmem((a_count * PAIR, 4 * PAIR), BF),
             pltpu.SMEM((a_count, NB), jnp.int32),
             pltpu.SMEM((KPTS,), jnp.int32),
@@ -403,10 +439,11 @@
             vmem((KPTS, KPTS), BF),
             vmem((a_count, ORB, NB, ORB), BF),
             vmem((NB, 2, PAIR, ORB * NB), BF),
+            vmem((k_count, a_count, 2, PAIR, LANES), BF),
             dma((2, 4, 2)), dma((2, 4, 2)), dma((2,)),
             dma((2, 4, 2)), dma((2, 4, 2)),
             dma((2, 2, 4, 2)), dma((2, 2, 4, 2)), dma((2, 2)),
-            dma((2, 2, 2)), dma((2, 2, 2)), dma((5,)),
+            dma((2, 2, 2)), dma((2, 2, 2)), dma((6,)),
             regular, regular,
         ],
         compiler_params=pltpu.CompilerParams(
@@ -426,6 +463,15 @@
             )
         )
     )
+    out = pl.pallas_call(
+        finish_kernel,
+        out_shape=shape,
+        in_specs=[in_vmem] * 3,
+        out_specs=hbm,
+        scratch_shapes=[vmem((2, a_count, PAIR, LANES), F32), dma((4,))],
+        compiler_params=pltpu.CompilerParams(vmem_limit_bytes=8 * 1024 * 1024),
+        name="finish",
+    )(most, last, k_inner)
     return out.reshape(k_count, a_count, components, e_count)
 
 

time: 62.8 us -> 61.6 us (0.981)
  local copies, waits for them, and re-layouts: 2.19 us -> 0 us
  Pallas kernels: 60.5 us -> 61.5 us
    unnamed x1 -> x0, local copies, waits for them, and re-layouts: 2.19 us -> none
    pallas_call x1 -> x2, Pallas kernels: 60.5 us -> 61.5 us  [the longest x1 59.3 us: shards(): pl.pallas_call(exchange_kernel, out_shape=(shape, jax.ShapeDtypeStruct((k...]
where the time goes in v5:
time: 61.6 us; the launch traced here: 61.5 us
  Pallas kernels  61.5 us (100%)
    pallas_call x1, Pallas kernels, shards(): pl.pallas_call(exchange_kernel, out_shape=(shape, jax.ShapeDtypeStruct((k...  59.3 us
    pallas_call x1, Pallas kernels, shards(): pl.pallas_call(finish_kernel, out_shape=shape, in_specs=[in_vmem] * 3, ou...  2.22 us

profile of v5, /device:TPU:1, one launch (start us, length us, event | category | flops | bytes accessed | tf_op | source)
XLA Modules:
  0.0 61.5 jit_solution(18251489298296976343)
XLA Ops:
  0.0 59.3 %exchange.1 = (f32[4,8,2,144,128]{4,3,2,1,0:T(8,128)S(1)}, bf16[4,2,4,144,128]{4,3,2,1,0:T(8,128)(2,1)S(1)}, bf16[1152,576]{1,0:T(8,128)(2,1)S(1)}) custom-call(bf16[4,8,2,144,128]{4,3,2,1,0:T(8,128)(2,1)} %bitcast.3, s32[8,8]{1,0:T(8,128)} %near_hbm.1, s32[16]{0:T(128)} %offsets_hbm.1, bf16[16,16]{1,0:T(8,128)(2,1)} %emit_hbm.1, bf16[16,16]{1,0:T(8,128)(2,1)} %absorb_hbm.1, ...), custom_call_target="tpu_custom_call" | custom-call | tf_op jit(solution)/shard_map/exchange/pallas_call | solution.py:413
  59.3 2.2 %finish.1 = f32[4,8,2,144,128]{4,3,2,1,0:T(8,128)} custom-call(f32[4,8,2,144,128]{4,3,2,1,0:T(8,128)S(1)} %get-tuple-element.8.most, bf16[4,2,4,144,128]{4,3,2,1,0:T(8,128)(2,1)S(1)} %get-tuple-element.9.last, bf16[1152,576]{1,0:T(8,128)(2,1)S(1)} %get-tuple-element.10.k_inner), custom_call_target="tpu_custom_call" | custom-call | tf_op jit(solution)/shard_map/finish/pallas_call | solution.py:466

commit v6 on v5

--- a/solution.py
+++ b/solution.py
@@ -211,55 +211,52 @@
         )
         return to_left, to_right
 
-    def home(chunk, half):
-        ks = pl.ds(2 * half, 2)
-        return outer.at[ks, zl, m + REACH] if chunk == 0 else inner.at[ks, zl, m]
-
-    def send_out(chunk, half, t, u):
+    def home(chunk):
+        return outer.at[:, zl, m + REACH] if chunk == 0 else inner.at[:, zl, m]
+
+    def send_out(chunk, t, u):
         m_to, zl_to = partner(t, u)
         return pltpu.make_async_remote_copy(
-            src_ref=made.at[chunk, pl.ds(m_to * 4 + 2 * half, 2), rows(zl_to), :],
-            dst_ref=home(chunk, half),
-            send_sem=out_send.at[chunk, half, t, u],
-            recv_sem=out_recv.at[chunk, half, t, u],
+            src_ref=made.at[chunk, pl.ds(m_to * 4, 4), rows(zl_to), :],
+            dst_ref=home(chunk),
+            send_sem=out_send.at[chunk, t, u],
+            recv_sem=out_recv.at[chunk, t, u],
             device_id=at(m_to, zl_to),
             device_id_type=MESH,
         )
 
-    def own_out(chunk, half):
+    def own_out(chunk):
         return pltpu.make_async_copy(
-            made.at[chunk, pl.ds(m * 4 + 2 * half, 2), rows(zl), :], home(chunk, half), out_local.at[chunk, half]
-        )
-
-    def landed(chunk, half, part):
+            made.at[chunk, pl.ds(m * 4, 4), rows(zl), :], home(chunk), out_local.at[chunk]
+        )
+
+    def landed(chunk, part):
         if part == 1:
             for t in range(4):
-                send_out(chunk, half, t, 1).wait_recv()
+                send_out(chunk, t, 1).wait_recv()
         else:
             for t in range(3):
-                send_out(chunk, half, t, 0).wait_recv()
-            own_out(chunk, half).wait()
+                send_out(chunk, t, 0).wait_recv()
+            own_out(chunk).wait()
 
     def c_of(part):
         return 1 - zl if part else zl
 
-    def y_copies(half, part):
-        ks, c = pl.ds(2 * half, 2), c_of(part)
+    def y_copies(part):
+        c = c_of(part)
         down = pltpu.make_async_remote_copy(
-            src_ref=outer.at[ks, c, pl.ds(2, 2)], dst_ref=outer.at[ks, c, pl.ds(6, 2)],
-            send_sem=y_send.at[half, part, 0], recv_sem=y_recv.at[half, part, 0],
-            device_id=y_left, device_id_type=MESH,
+            src_ref=outer.at[:, c, pl.ds(2, 2)], dst_ref=outer.at[:, c, pl.ds(6, 2)],
+            send_sem=y_send.at[part, 0], recv_sem=y_recv.at[part, 0], device_id=y_left, device_id_type=MESH,
         )
         up = pltpu.make_async_remote_copy(
-            src_ref=outer.at[ks, c, pl.ds(4, 2)], dst_ref=outer.at[ks, c, pl.ds(0, 2)],
-            send_sem=y_send.at[half, part, 1], recv_sem=y_recv.at[half, part, 1],
-            device_id=y_right, device_id_type=MESH,
+            src_ref=outer.at[:, c, pl.ds(4, 2)], dst_ref=outer.at[:, c, pl.ds(0, 2)],
+            send_sem=y_send.at[part, 1], recv_sem=y_recv.at[part, 1], device_id=y_right, device_id_type=MESH,
         )
         return down, up
 
-    def spread(half, part):
-        landed(0, half, part)
-        for copy in y_copies(half, part):
+    def spread(part):
+        landed(0, part)
+        for copy in y_copies(part):
             copy.start()
 
     for chunk in range(2):
@@ -278,15 +275,13 @@
             right_out[chunk, group] = (packed[PAIR:, LANES:] * keep_right).astype(BF)
             for copy in edge_copies(chunk, t):
                 copy.start()
-        if chunk == 1:
-            spread(0, 0)
         for t in range(4):
             for copy in edge_copies(chunk, t):
                 copy.wait()
 
         @pl.loop(0, 8)
         def _(turn):
-            half, t = turn // 4, turn % 4
+            half, t = turn % 2, turn // 2
             m_to, _ = partner(t, 0)
             kp = m_to * 2 + half
             start = KPTS - 2 * kp
@@ -304,35 +299,32 @@
             made[chunk, 2 * kp] = total[:, :LANES]
             made[chunk, 2 * kp + 1] = total[:, LANES:]
 
-            @pl.when(t < 3)
+            @pl.when((half == 1) & (t < 3))
             def _():
-                send_out(chunk, half, t, 0).start()
-
-            @pl.when(t == 3)
+                send_out(chunk, t, 0).start()
+
+            @pl.when(turn == 7)
             def _():
-                own_out(chunk, half).start()
+                own_out(chunk).start()
                 for near_t in range(4):
-                    send_out(chunk, half, near_t, 1).start()
+                    send_out(chunk, near_t, 1).start()
 
             if chunk == 1:
 
-                @pl.when(turn == 0)
+                @pl.when(turn == 1)
                 def _():
-                    spread(0, 1)
-
-                @pl.when(turn == 5)
-                def _():
-                    spread(1, 0)
-
-    spread(1, 1)
+                    spread(0)
+
+    spread(1)
 
     def pair_of(source, half, c, first):
         two = [source[2 * half + j, c, pl.ds(first, 4)].reshape(4 * PAIR, LANES) for j in range(2)]
         return jnp.concatenate(two, axis=1)
 
     def apply_outer(half, part):
-        for copy in y_copies(half, part):
-            copy.wait()
+        if half == 0:
+            for copy in y_copies(part):
+                copy.wait()
         c = c_of(part)
 
         @pl.loop(0, 2)
@@ -346,7 +338,8 @@
                         out[2 * half + j, a + i, c] = block[i * PAIR : (i + 1) * PAIR, j * LANES : (j + 1) * LANES]
 
     def apply_inner(half, part):
-        landed(1, half, part)
+        if half == 0:
+            landed(1, part)
         c = c_of(part)
 
         @pl.loop(0, 2)
@@ -359,45 +352,39 @@
                     for j in range(2):
                         out[2 * half + j, a + i, c] += block[i * PAIR : (i + 1) * PAIR, j * LANES : (j + 1) * LANES]
 
-    apply_outer(0, 0)
-    apply_outer(0, 1)
-    apply_inner(0, 0)
-    apply_outer(1, 0)
-    apply_inner(0, 1)
-    apply_outer(1, 1)
-    apply_inner(1, 0)
-    landed(1, 1, 1)
+    for half in range(2):
+        apply_outer(half, 0)
+    for half in range(2):
+        apply_inner(half, 0)
+    for half in range(2):
+        apply_outer(half, 1)
+    landed(1, 1)
     for chunk in range(2):
         for t, u in steps:
             send_in(chunk, t, u).wait_send()
     for chunk in range(2):
-        for half in range(2):
-            for t, u in steps:
-                send_out(chunk, half, t, u).wait_send()
+        for t, u in steps:
+            send_out(chunk, t, u).wait_send()
 
 
 def finish_kernel(most, last, k_inner, out, block, sems):
     c = 1 - lax.axis_index("energy") % 2
-    first = pl.ds(0, 2)
-    second = pl.ds(2, 2)
-    copies = [
-        pltpu.make_async_copy(most.at[first], out.at[first], sems.at[0]),
-        pltpu.make_async_copy(most.at[second, :, 1 - c], out.at[second, :, 1 - c], sems.at[1]),
-    ]
-    for copy in copies:
-        copy.start()
-    operand = jnp.concatenate([last[2 + j, c].reshape(4 * PAIR, LANES) for j in range(2)], axis=1)
-    for side in range(2):
-        for part in range(2):
-            a = 4 * side + 2 * part
-            product = jnp.dot(k_inner[a * PAIR : (a + 2) * PAIR, :], operand, preferred_element_type=F32)
-            for i in range(2):
-                for j in range(2):
-                    block[j, a + i] = most[2 + j, a + i, c] + product[i * PAIR : (i + 1) * PAIR, j * LANES : (j + 1) * LANES]
-        atoms = pl.ds(4 * side, 4)
-        copy = pltpu.make_async_copy(block.at[:, atoms], out.at[second, atoms, c], sems.at[2 + side])
-        copy.start()
-        copies.append(copy)
+    copies = [pltpu.make_async_copy(most.at[:, :, 1 - c], out.at[:, :, 1 - c], sems.at[0])]
+    copies[0].start()
+    for half in range(2):
+        operand = jnp.concatenate([last[2 * half + j, c].reshape(4 * PAIR, LANES) for j in range(2)], axis=1)
+        for side in range(2):
+            for part in range(2):
+                a = 4 * side + 2 * part
+                product = jnp.dot(k_inner[a * PAIR : (a + 2) * PAIR, :], operand, preferred_element_type=F32)
+                for i in range(2):
+                    for j in range(2):
+                        k = 2 * half + j
+                        block[k, a + i] = most[k, a + i, c] + product[i * PAIR : (i + 1) * PAIR, j * LANES : (j + 1) * LANES]
+            ks, atoms = pl.ds(2 * half, 2), pl.ds(4 * side, 4)
+            copy = pltpu.make_async_copy(block.at[ks, atoms], out.at[ks, atoms, c], sems.at[1 + 2 * half + side])
+            copy.start()
+            copies.append(copy)
     for copy in copies:
         copy.wait()
 
@@ -442,8 +429,8 @@
             vmem((k_count, a_count, 2, PAIR, LANES), BF),
             dma((2, 4, 2)), dma((2, 4, 2)), dma((2,)),
             dma((2, 4, 2)), dma((2, 4, 2)),
-            dma((2, 2, 4, 2)), dma((2, 2, 4, 2)), dma((2, 2)),
-            dma((2, 2, 2)), dma((2, 2, 2)), dma((6,)),
+            dma((2, 4, 2)), dma((2, 4, 2)), dma((2,)),
+            dma((2, 2)), dma((2, 2)), dma((6,)),
             regular, regular,
         ],
         compiler_params=pltpu.CompilerParams(
@@ -468,7 +455,7 @@
         out_shape=shape,
         in_specs=[in_vmem] * 3,
         out_specs=hbm,
-        scratch_shapes=[vmem((2, a_count, PAIR, LANES), F32), dma((4,))],
+        scratch_shapes=[vmem((k_count, a_count, PAIR, LANES), F32), dma((5,))],
         compiler_params=pltpu.CompilerParams(vmem_limit_bytes=8 * 1024 * 1024),
         name="finish",
     )(most, last, k_inner)

time: 61.6 us -> 61.8 us (level)
  no operation moved by 1% of the time
where the time goes in v6:
time: 61.8 us; the launch traced here: 61.7 us
  Pallas kernels  61.7 us (100%)
    pallas_call x1, Pallas kernels, shards(): pl.pallas_call(exchange_kernel, out_shape=(shape, jax.ShapeDtypeStruct((k...  59.3 us
    pallas_call x1, Pallas kernels, shards(): pl.pallas_call(finish_kernel, out_shape=shape, in_specs=[in_vmem] * 3, ou...  2.39 us

profile of v6, /device:TPU:1, one launch (start us, length us, event | category | flops | bytes accessed | tf_op | source)
XLA Modules:
  0.0 61.7 jit_solution(12629799347107912731)
XLA Ops:
  0.0 59.3 %exchange.1 = (f32[4,8,2,144,128]{4,3,2,1,0:T(8,128)S(1)}, bf16[4,2,4,144,128]{4,3,2,1,0:T(8,128)(2,1)S(1)}, bf16[1152,576]{1,0:T(8,128)(2,1)S(1)}) custom-call(bf16[4,8,2,144,128]{4,3,2,1,0:T(8,128)(2,1)} %bitcast.3, s32[8,8]{1,0:T(8,128)} %near_hbm.1, s32[16]{0:T(128)} %offsets_hbm.1, bf16[16,16]{1,0:T(8,128)(2,1)} %emit_hbm.1, bf16[16,16]{1,0:T(8,128)(2,1)} %absorb_hbm.1, ...), custom_call_target="tpu_custom_call" | custom-call | tf_op jit(solution)/shard_map/exchange/pallas_call | solution.py:400
  59.3 2.4 %finish.1 = f32[4,8,2,144,128]{4,3,2,1,0:T(8,128)} custom-call(f32[4,8,2,144,128]{4,3,2,1,0:T(8,128)S(1)} %get-tuple-element.8.most, bf16[4,2,4,144,128]{4,3,2,1,0:T(8,128)(2,1)S(1)} %get-tuple-element.9.last, bf16[1152,576]{1,0:T(8,128)(2,1)S(1)} %get-tuple-element.10.k_inner), custom_call_target="tpu_custom_call" | custom-call | tf_op jit(solution)/shard_map/finish/pallas_call | solution.py:453

commit v7 on v5

--- a/solution.py
+++ b/solution.py
@@ -112,7 +112,7 @@
         )
 
     for chunk in range(2):
-        for t, u in steps:
+        for t, u in ((0, 0), (3, 1), (0, 1), (1, 0), (2, 1), (1, 1), (2, 0)):
             send_in(chunk, t, u).start()
         own_in(chunk).start()
     for copy in fetches:
@@ -378,11 +378,12 @@
 
 def finish_kernel(most, last, k_inner, out, block, sems):
     c = 1 - lax.axis_index("energy") % 2
-    first = pl.ds(0, 2)
     second = pl.ds(2, 2)
     copies = [
-        pltpu.make_async_copy(most.at[first], out.at[first], sems.at[0]),
-        pltpu.make_async_copy(most.at[second, :, 1 - c], out.at[second, :, 1 - c], sems.at[1]),
+        pltpu.make_async_copy(most.at[0], out.at[0], sems.at[0]),
+        pltpu.make_async_copy(most.at[1], out.at[1], sems.at[4]),
+        pltpu.make_async_copy(most.at[2, :, 1 - c], out.at[2, :, 1 - c], sems.at[1]),
+        pltpu.make_async_copy(most.at[3, :, 1 - c], out.at[3, :, 1 - c], sems.at[5]),
     ]
     for copy in copies:
         copy.start()
@@ -468,7 +469,7 @@
         out_shape=shape,
         in_specs=[in_vmem] * 3,
         out_specs=hbm,
-        scratch_shapes=[vmem((2, a_count, PAIR, LANES), F32), dma((4,))],
+        scratch_shapes=[vmem((2, a_count, PAIR, LANES), F32), dma((6,))],
         compiler_params=pltpu.CompilerParams(vmem_limit_bytes=8 * 1024 * 1024),
         name="finish",
     )(most, last, k_inner)

time: 61.6 us -> 61.6 us (level)
  no operation moved by 1% of the time
where the time goes in v7:
time: 61.6 us; the launch traced here: 61.5 us
  Pallas kernels  61.5 us (100%)
    pallas_call x1, Pallas kernels, shards(): pl.pallas_call(exchange_kernel, out_shape=(shape, jax.ShapeDtypeStruct((k...  59.2 us
    pallas_call x1, Pallas kernels, shards(): pl.pallas_call(finish_kernel, out_shape=shape, in_specs=[in_vmem] * 3, ou...  2.24 us

profile of v7, /device:TPU:1, one launch (start us, length us, event | category | flops | bytes accessed | tf_op | source)
XLA Modules:
  0.0 61.5 jit_solution(11422662291947869999)
XLA Ops:
  0.0 59.2 %exchange.1 = (f32[4,8,2,144,128]{4,3,2,1,0:T(8,128)S(1)}, bf16[4,2,4,144,128]{4,3,2,1,0:T(8,128)(2,1)S(1)}, bf16[1152,576]{1,0:T(8,128)(2,1)S(1)}) custom-call(bf16[4,8,2,144,128]{4,3,2,1,0:T(8,128)(2,1)} %bitcast.3, s32[8,8]{1,0:T(8,128)} %near_hbm.1, s32[16]{0:T(128)} %offsets_hbm.1, bf16[16,16]{1,0:T(8,128)(2,1)} %emit_hbm.1, bf16[16,16]{1,0:T(8,128)(2,1)} %absorb_hbm.1, ...), custom_call_target="tpu_custom_call" | custom-call | tf_op jit(solution)/shard_map/exchange/pallas_call | solution.py:414
  59.2 2.2 %finish.1 = f32[4,8,2,144,128]{4,3,2,1,0:T(8,128)} custom-call(f32[4,8,2,144,128]{4,3,2,1,0:T(8,128)S(1)} %get-tuple-element.8.most, bf16[4,2,4,144,128]{4,3,2,1,0:T(8,128)(2,1)S(1)} %get-tuple-element.9.last, bf16[1152,576]{1,0:T(8,128)(2,1)S(1)} %get-tuple-element.10.k_inner), custom_call_target="tpu_custom_call" | custom-call | tf_op jit(solution)/shard_map/finish/pallas_call | solution.py:467

commit v8 on v5

--- a/solution.py
+++ b/solution.py
@@ -65,8 +65,6 @@
 
     barrier = pltpu.get_barrier_semaphore()
     steps = [(t, u) for t in range(4) for u in range(2) if (t, u) != (3, 0)]
-    prefetch = pltpu.make_async_copy(green_hbm, green, small.at[5])
-    prefetch.start()
     sides = (x_left, x_right, y_left, y_right)
     head = m * 2 + zl == 0
     for t, u in steps:
@@ -78,6 +76,8 @@
         for side in sides:
             pl.semaphore_signal(barrier, inc=1, device_id=side, device_id_type=MESH)
 
+    prefetch = pltpu.make_async_copy(green_hbm, green, small.at[5])
+    prefetch.start()
     fetches = [
         pltpu.make_async_copy(src, dst, small.at[i])
         for i, (src, dst) in enumerate(

time: 61.6 us -> 61.6 us (level)
  no operation moved by 1% of the time
where the time goes in v8:
time: 61.6 us; the launch traced here: 61.5 us
  Pallas kernels  61.5 us (100%)
    pallas_call x1, Pallas kernels, shards(): pl.pallas_call(exchange_kernel, out_shape=(shape, jax.ShapeDtypeStruct((k...  59.3 us
    pallas_call x1, Pallas kernels, shards(): pl.pallas_call(finish_kernel, out_shape=shape, in_specs=[in_vmem] * 3, ou...  2.22 us

profile of v8, /device:TPU:1, one launch (start us, length us, event | category | flops | bytes accessed | tf_op | source)
XLA Modules:
  0.0 61.5 jit_solution(15831426220421401406)
XLA Ops:
  0.0 59.3 %exchange.1 = (f32[4,8,2,144,128]{4,3,2,1,0:T(8,128)S(1)}, bf16[4,2,4,144,128]{4,3,2,1,0:T(8,128)(2,1)S(1)}, bf16[1152,576]{1,0:T(8,128)(2,1)S(1)}) custom-call(bf16[4,8,2,144,128]{4,3,2,1,0:T(8,128)(2,1)} %bitcast.3, s32[8,8]{1,0:T(8,128)} %near_hbm.1, s32[16]{0:T(128)} %offsets_hbm.1, bf16[16,16]{1,0:T(8,128)(2,1)} %emit_hbm.1, bf16[16,16]{1,0:T(8,128)(2,1)} %absorb_hbm.1, ...), custom_call_target="tpu_custom_call" | custom-call | tf_op jit(solution)/shard_map/exchange/pallas_call | solution.py:413
  59.3 2.2 %finish.1 = f32[4,8,2,144,128]{4,3,2,1,0:T(8,128)} custom-call(f32[4,8,2,144,128]{4,3,2,1,0:T(8,128)S(1)} %get-tuple-element.8.most, bf16[4,2,4,144,128]{4,3,2,1,0:T(8,128)(2,1)S(1)} %get-tuple-element.9.last, bf16[1152,576]{1,0:T(8,128)(2,1)S(1)} %get-tuple-element.10.k_inner), custom_call_target="tpu_custom_call" | custom-call | tf_op jit(solution)/shard_map/finish/pallas_call | solution.py:466
